TPU v7x, 1024 devices: a whole 4x8x16 slice. The times are simulated.
1024 devices in a mesh: rad: 64 (over y, z_lo, core), azi: 16 (over x, z_hi).
Axes of the slice: x: 4, y: 8, z: 16 (z_hi: 4, z_lo: 4; z = z_hi * 4 + z_lo), core: 2. Of those that a mesh axis runs over, the one named last changes fastest.
Arguments:
- state: float32 [5, 4, 1024, 2048], P(None, None, 'rad', 'azi'), may hold values from -6 to 6
- shifts: int32 [1024], replicated, may hold values from 0 to 2047
- spin: float32 [1024], replicated, may hold values from 0.2 to 1
- drift: float32 [1024], replicated, may hold values from -1.5 to 1.5
- stiffness: float32 [4, 1024], replicated, may hold values from 0.5 to 2
Outputs:
- evolved: float32 [5, 4, 1024, 2048], P(None, None, 'rad', 'azi')
All inputs are finite; a program needn't handle non-finite values.
Results may differ from a plain program's by a relative error of at most 0.00002.
Values sent between devices are 32-bit elements; how exact they have to be, the bound alone decides.
No kernel may reach another device: no remote copies, remote signals or barrier semaphores. Data moves between devices by JAX's collectives and lax.ppermute only.
A program may use at most 32 MiB of HBM per device.

v0:
```python
import jax
import jax.numpy as jnp
from jax import lax
from jax.sharding import PartitionSpec as P

STEPS = 2


time_step = 0.15
diffuse = 0.05


def extended_2(block, sides, width, periodic):
    for axis, dim in sides:
        count = lax.axis_size(axis)
        forward = [(i, i + 1) for i in range(count - 1)]
        if periodic:
            forward.append((count - 1, 0))
        backward = [(target, source) for source, target in forward]
        low = lax.ppermute(
            lax.slice_in_dim(block, block.shape[dim] - width, None, axis=dim), axis, forward
        )
        high = lax.ppermute(lax.slice_in_dim(block, 0, width, axis=dim), axis, backward)
        block = jnp.concatenate([low, block, high], axis=dim)
    return block


def from_behind(block, axis, distance):
    devices = range(lax.axis_size(axis))
    route = [((i - distance) % len(devices), i) for i in devices]
    return lax.ppermute(block, axis, route)


def tendency(extended, stiff_rows, spin_rows, drift_rows):
    centre_cells = extended[:, :, 1:-1, 1:-1]
    upper_row = extended[:, :, 2:, 1:-1]
    lower_row = extended[:, :, :-2, 1:-1]
    ahead_cell = extended[:, :, 1:-1, 2:]
    behind_cell = extended[:, :, 1:-1, :-2]
    rad_slope = 0.5 * (upper_row - lower_row)
    azi_slope = 0.5 * (ahead_cell - behind_cell)
    laplace_sum = upper_row + lower_row + ahead_cell + behind_cell - 4.0 * centre_cells
    vertical_pad = jnp.pad(centre_cells[3:5], ((0, 0), (1, 1), (0, 0), (0, 0)))
    ver_slope = 0.5 * (vertical_pad[:, 2:] - vertical_pad[:, :-2])
    spin_col = spin_rows[:, None]
    drift_col = drift_rows[:, None]
    divergence = rad_slope[1] + azi_slope[2] + ver_slope[0]
    coupled = jnp.stack(
        [
            -divergence,
            2.0 * spin_col * centre_cells[2] - rad_slope[4],
            -0.5 * spin_col * centre_cells[1] - azi_slope[4],
            -ver_slope[1],
            -stiff_rows[:, :, None] * divergence,
        ]
    )
    return coupled - drift_col * azi_slope + diffuse * laplace_sum


def barrel_roll(block, amounts, length):
    result = block
    for bit_index in range((length - 1).bit_length()):
        taken = amounts // (1 << bit_index) % 2 == 1
        result = jnp.where(taken[None, :, None], jnp.roll(result, 1 << bit_index, axis=2), result)
    return result


def on_device(state, shifts, spin, drift, stiffness):
    planes, levels, rows, cells = state.shape
    rad_start = lax.axis_index("rad") * rows

    def rows_of(values, offset, count):
        padded = jnp.pad(values, [(0, 0)] * (values.ndim - 1) + [(3, 3)])
        return lax.dynamic_slice_in_dim(padded, rad_start + offset + 3, count, axis=values.ndim - 1)

    def coefs(offset, count):
        return (
            rows_of(stiffness, offset, count),
            rows_of(spin, offset, count),
            rows_of(drift, offset, count),
        )

    def operator(field):
        extended = extended_2(field, (("rad", 2),), 1, False)
        extended = extended_2(extended, (("azi", 3),), 1, True)
        return tendency(extended, *coefs(0, rows))

    local_shifts = rows_of(shifts, 0, rows)
    current = state
    for step_index in range(STEPS):
        first = current + time_step * operator(current)
        second = 0.75 * current + 0.25 * (first + time_step * operator(first))
        sectioned = current / 3.0 + 2.0 / 3.0 * (second + time_step * operator(second))
        flat = sectioned.reshape(planes * levels, rows, cells)
        tile_count = lax.axis_size("azi")
        hops = local_shifts // cells
        offsets = local_shifts % cells
        moved = flat
        for bit_index in range(tile_count.bit_length() - 1):
            arrived = from_behind(moved, "azi", 1 << bit_index)
            taken = hops // (1 << bit_index) % 2 == 1
            moved = jnp.where(taken[None, :, None], arrived, moved)
        before = from_behind(moved, "azi", 1)
        paired = jnp.concatenate([before, moved], axis=2)
        flat = barrel_roll(paired, offsets, cells)[:, :, cells:]
        current = flat.reshape(planes, levels, rows, cells)
    return current


def solution(mesh):
    in_specs = (P(None, None, "rad", "azi"), P(), P(), P(), P())
    out_specs = P(None, None, "rad", "azi")
    return jax.shard_map(
        on_device, mesh=mesh, in_specs=in_specs, out_specs=out_specs, check_vma=False
    )
```

profile of v0, /device:TPU:8, one launch (start us, length us, event | category | flops | bytes accessed | tf_op | source)
XLA Modules:
  0.0 428.4 jit_solution(5966322789508936183)
XLA Ops:
  2.9 7.2 %collective-permute-start = (f32[5,4,1,128]{3,2,1,0:T(1,128)S(1)}, f32[5,4,1,128]{3,2,1,0:T(1,128)S(1)}, u32[]{:S(2)}, u32[]{:S(2)}) collective-permute-start(f32[5,4,1,128]{3,2,1,0:T(1,128)S(1)} %get-tuple-element.45), channel_id=1, source_target_pairs={{16,0},{32,16},{48,32},{64,48},{80,64},{96,80},{112,96},{128,112},... | collective-permute-start | bytes 30728 | tf_op jit(solution)/shard_map/ppermute | solution.py:23
  12.0 10.9 %collective-permute-start.3 = (f32[5,4,18,1]{3,2,1,0:T(8,128)S(1)}, f32[5,4,18,1]{3,2,1,0:T(8,128)S(1)}, u32[]{:S(2)}, u32[]{:S(2)}) collective-permute-start(f32[5,4,18,1]{3,2,1,0:T(8,128)S(1)} %get-tuple-element.20), channel_id=1, source_target_pairs={{0,1},{1,2},{2,3},{3,4},{4,5},{5,6},{6,7},{7,8},{8,9},{9,10},{10,1... | collective-permute-start | bytes 4328 | tf_op jit(solution)/shard_map/ppermute | solution.py:20
  22.9 10.5 %collective-permute-start.2 = (f32[5,4,18,1]{3,2,1,0:T(8,128)S(1)}, f32[5,4,18,1]{3,2,1,0:T(8,128)S(1)}, u32[]{:S(2)}, u32[]{:S(2)}) collective-permute-start(f32[5,4,18,1]{3,2,1,0:T(8,128)S(1)} %get-tuple-element.21), channel_id=1, source_target_pairs={{1,0},{2,1},{3,2},{4,3},{5,4},{6,5},{7,6},{8,7},{9,8},{10,9},{11,1... | collective-permute-start | bytes 4328 | tf_op jit(solution)/shard_map/ppermute | solution.py:23
  36.9 16.4 %collective-permute-done.2 = f32[5,4,18,1]{3,2,1,0:T(8,128)S(1)} collective-permute-done((f32[5,4,18,1]{3,2,1,0:T(8,128)S(1)}, f32[5,4,18,1]{3,2,1,0:T(8,128)S(1)}, u32[]{:S(2)}, u32[]{:S(2)}) %collective-permute-start.2) | collective-permute-done | bytes 1472 | tf_op jit(solution)/shard_map/ppermute | solution.py:23
  56.0 6.3 %collective-permute-start.4 = (f32[5,4,1,128]{3,2,1,0:T(1,128)S(1)}, f32[5,4,1,128]{3,2,1,0:T(1,128)S(1)}, u32[]{:S(2)}, u32[]{:S(2)}) collective-permute-start(f32[5,4,1,128]{3,2,1,0:T(1,128)S(1)} %get-tuple-element.43), channel_id=1, source_target_pairs={{16,0},{32,16},{48,32},{64,48},{80,64},{96,80},{112,96},{128,112},... | collective-permute-start | bytes 30728 | tf_op jit(solution)/shard_map/ppermute | solution.py:23
  63.9 6.8 %collective-permute-start.7 = (f32[5,4,18,1]{3,2,1,0:T(8,128)S(1)}, f32[5,4,18,1]{3,2,1,0:T(8,128)S(1)}, u32[]{:S(2)}, u32[]{:S(2)}) collective-permute-start(f32[5,4,18,1]{3,2,1,0:T(8,128)S(1)} %get-tuple-element.18), channel_id=1, source_target_pairs={{0,1},{1,2},{2,3},{3,4},{4,5},{5,6},{6,7},{7,8},{8,9},{9,10},{10,1... | collective-permute-start | bytes 4328 | tf_op jit(solution)/shard_map/ppermute | solution.py:20
  70.7 5.6 %collective-permute-start.6 = (f32[5,4,18,1]{3,2,1,0:T(8,128)S(1)}, f32[5,4,18,1]{3,2,1,0:T(8,128)S(1)}, u32[]{:S(2)}, u32[]{:S(2)}) collective-permute-start(f32[5,4,18,1]{3,2,1,0:T(8,128)S(1)} %get-tuple-element.19), channel_id=1, source_target_pairs={{1,0},{2,1},{3,2},{4,3},{5,4},{6,5},{7,6},{8,7},{9,8},{10,9},{11,1... | collective-permute-start | bytes 4328 | tf_op jit(solution)/shard_map/ppermute | solution.py:23
  79.1 7.4 %collective-permute-done.6 = f32[5,4,18,1]{3,2,1,0:T(8,128)S(1)} collective-permute-done((f32[5,4,18,1]{3,2,1,0:T(8,128)S(1)}, f32[5,4,18,1]{3,2,1,0:T(8,128)S(1)}, u32[]{:S(2)}, u32[]{:S(2)}) %collective-permute-start.6) | collective-permute-done | bytes 1472 | tf_op jit(solution)/shard_map/ppermute | solution.py:23
  89.3 15.5 %collective-permute-start.8 = (f32[5,4,1,128]{3,2,1,0:T(1,128)S(1)}, f32[5,4,1,128]{3,2,1,0:T(1,128)S(1)}, u32[]{:S(2)}, u32[]{:S(2)}) collective-permute-start(f32[5,4,1,128]{3,2,1,0:T(1,128)S(1)} %get-tuple-element.41), channel_id=1, source_target_pairs={{16,0},{32,16},{48,32},{64,48},{80,64},{96,80},{112,96},{128,112},... | collective-permute-start | bytes 30728 | tf_op jit(solution)/shard_map/ppermute | solution.py:23
  110.1 8.2 %collective-permute-start.10 = (f32[5,4,18,1]{3,2,1,0:T(8,128)S(1)}, f32[5,4,18,1]{3,2,1,0:T(8,128)S(1)}, u32[]{:S(2)}, u32[]{:S(2)}) collective-permute-start(f32[5,4,18,1]{3,2,1,0:T(8,128)S(1)} %get-tuple-element.17), channel_id=1, source_target_pairs={{1,0},{2,1},{3,2},{4,3},{5,4},{6,5},{7,6},{8,7},{9,8},{10,9},{11,1... | collective-permute-start | bytes 4328 | tf_op jit(solution)/shard_map/ppermute | solution.py:23
  118.3 12.0 %collective-permute-done.11 = f32[5,4,18,1]{3,2,1,0:T(8,128)S(1)} collective-permute-done((f32[5,4,18,1]{3,2,1,0:T(8,128)S(1)}, f32[5,4,18,1]{3,2,1,0:T(8,128)S(1)}, u32[]{:S(2)}, u32[]{:S(2)}) %collective-permute-start.11) | collective-permute-done | bytes 1472 | tf_op jit(solution)/shard_map/ppermute | solution.py:20
  137.4 26.4 %collective-permute-done.12 = f32[20,16,128]{2,1,0:T(8,128)S(1)} collective-permute-done((f32[20,16,128]{2,1,0:T(8,128)S(1)}, f32[20,16,128]{2,1,0:T(8,128)S(1)}, u32[]{:S(2)}, u32[]{:S(2)}) %collective-permute-start.12) | collective-permute-done | bytes 163872 | tf_op jit(solution)/shard_map/ppermute | solution.py:31
  165.8 22.0 %collective-permute-done.13 = f32[20,16,128]{2,1,0:T(8,128)S(1)} collective-permute-done((f32[20,16,128]{2,1,0:T(8,128)S(1)}, f32[20,16,128]{2,1,0:T(8,128)S(1)}, u32[]{:S(2)}, u32[]{:S(2)}) %collective-permute-start.13) | collective-permute-done | bytes 163872 | tf_op jit(solution)/shard_map/ppermute | solution.py:31
  189.8 7.3 %collective-permute-done.14 = f32[20,16,128]{2,1,0:T(8,128)S(1)} collective-permute-done((f32[20,16,128]{2,1,0:T(8,128)S(1)}, f32[20,16,128]{2,1,0:T(8,128)S(1)}, u32[]{:S(2)}, u32[]{:S(2)}) %collective-permute-start.14) | collective-permute-done | bytes 163872 | tf_op jit(solution)/shard_map/ppermute | solution.py:31
  199.1 6.8 %collective-permute-done.15 = f32[20,16,128]{2,1,0:T(8,128)S(1)} collective-permute-done((f32[20,16,128]{2,1,0:T(8,128)S(1)}, f32[20,16,128]{2,1,0:T(8,128)S(1)}, u32[]{:S(2)}, u32[]{:S(2)}) %collective-permute-start.15) | collective-permute-done | bytes 163872 | tf_op jit(solution)/shard_map/ppermute | solution.py:31
  208.1 12.2 %collective-permute-done.16 = f32[20,16,128]{2,1,0:T(8,128)S(1)} collective-permute-done((f32[20,16,128]{2,1,0:T(8,128)S(1)}, f32[20,16,128]{2,1,0:T(8,128)S(1)}, u32[]{:S(2)}, u32[]{:S(2)}) %collective-permute-start.16) | collective-permute-done | bytes 163872 | tf_op jit(solution)/shard_map/ppermute | solution.py:31
  224.1 6.3 %collective-permute-start.17 = (f32[5,4,1,128]{3,2,1,0:T(1,128)S(1)}, f32[5,4,1,128]{3,2,1,0:T(1,128)S(1)}, u32[]{:S(2)}, u32[]{:S(2)}) collective-permute-start(f32[5,4,1,128]{3,2,1,0:T(1,128)S(1)} %get-tuple-element.39), channel_id=1, source_target_pairs={{16,0},{32,16},{48,32},{64,48},{80,64},{96,80},{112,96},{128,112},... | collective-permute-start | bytes 30728 | tf_op jit(solution)/shard_map/ppermute | solution.py:23
  233.9 9.9 %collective-permute-start.19 = (f32[5,4,18,1]{3,2,1,0:T(8,128)S(1)}, f32[5,4,18,1]{3,2,1,0:T(8,128)S(1)}, u32[]{:S(2)}, u32[]{:S(2)}) collective-permute-start(f32[5,4,18,1]{3,2,1,0:T(8,128)S(1)} %get-tuple-element.15), channel_id=1, source_target_pairs={{1,0},{2,1},{3,2},{4,3},{5,4},{6,5},{7,6},{8,7},{9,8},{10,9},{11,1... | collective-permute-start | bytes 4328 | tf_op jit(solution)/shard_map/ppermute | solution.py:23
  243.9 10.9 %collective-permute-done.20 = f32[5,4,18,1]{3,2,1,0:T(8,128)S(1)} collective-permute-done((f32[5,4,18,1]{3,2,1,0:T(8,128)S(1)}, f32[5,4,18,1]{3,2,1,0:T(8,128)S(1)}, u32[]{:S(2)}, u32[]{:S(2)}) %collective-permute-start.20) | collective-permute-done | bytes 1472 | tf_op jit(solution)/shard_map/ppermute | solution.py:20
  254.7 6.6 %collective-permute-done.19 = f32[5,4,18,1]{3,2,1,0:T(8,128)S(1)} collective-permute-done((f32[5,4,18,1]{3,2,1,0:T(8,128)S(1)}, f32[5,4,18,1]{3,2,1,0:T(8,128)S(1)}, u32[]{:S(2)}, u32[]{:S(2)}) %collective-permute-start.19) | collective-permute-done | bytes 1472 | tf_op jit(solution)/shard_map/ppermute | solution.py:23
  264.1 6.3 %collective-permute-start.21 = (f32[5,4,1,128]{3,2,1,0:T(1,128)S(1)}, f32[5,4,1,128]{3,2,1,0:T(1,128)S(1)}, u32[]{:S(2)}, u32[]{:S(2)}) collective-permute-start(f32[5,4,1,128]{3,2,1,0:T(1,128)S(1)} %get-tuple-element.37), channel_id=1, source_target_pairs={{16,0},{32,16},{48,32},{64,48},{80,64},{96,80},{112,96},{128,112},... | collective-permute-start | bytes 30728 | tf_op jit(solution)/shard_map/ppermute | solution.py:23
  276.4 9.5 %collective-permute-start.23 = (f32[5,4,18,1]{3,2,1,0:T(8,128)S(1)}, f32[5,4,18,1]{3,2,1,0:T(8,128)S(1)}, u32[]{:S(2)}, u32[]{:S(2)}) collective-permute-start(f32[5,4,18,1]{3,2,1,0:T(8,128)S(1)} %get-tuple-element.13), channel_id=1, source_target_pairs={{1,0},{2,1},{3,2},{4,3},{5,4},{6,5},{7,6},{8,7},{9,8},{10,9},{11,1... | collective-permute-start | bytes 4328 | tf_op jit(solution)/shard_map/ppermute | solution.py:23
  285.9 14.6 %collective-permute-done.24 = f32[5,4,18,1]{3,2,1,0:T(8,128)S(1)} collective-permute-done((f32[5,4,18,1]{3,2,1,0:T(8,128)S(1)}, f32[5,4,18,1]{3,2,1,0:T(8,128)S(1)}, u32[]{:S(2)}, u32[]{:S(2)}) %collective-permute-start.24) | collective-permute-done | bytes 1472 | tf_op jit(solution)/shard_map/ppermute | solution.py:20
  303.2 6.3 %collective-permute-start.25 = (f32[5,4,1,128]{3,2,1,0:T(1,128)S(1)}, f32[5,4,1,128]{3,2,1,0:T(1,128)S(1)}, u32[]{:S(2)}, u32[]{:S(2)}) collective-permute-start(f32[5,4,1,128]{3,2,1,0:T(1,128)S(1)} %get-tuple-element.35), channel_id=1, source_target_pairs={{16,0},{32,16},{48,32},{64,48},{80,64},{96,80},{112,96},{128,112},... | collective-permute-start | bytes 30728 | tf_op jit(solution)/shard_map/ppermute | solution.py:23
  309.6 7.1 %collective-permute-done.26 = f32[5,4,1,128]{3,2,1,0:T(1,128)S(1)} collective-permute-done((f32[5,4,1,128]{3,2,1,0:T(1,128)S(1)}, f32[5,4,1,128]{3,2,1,0:T(1,128)S(1)}, u32[]{:S(2)}, u32[]{:S(2)}) %collective-permute-start.26) | collective-permute-done | bytes 10272 | tf_op jit(solution)/shard_map/ppermute | solution.py:20
  319.7 9.1 %collective-permute-start.27 = (f32[5,4,18,1]{3,2,1,0:T(8,128)S(1)}, f32[5,4,18,1]{3,2,1,0:T(8,128)S(1)}, u32[]{:S(2)}, u32[]{:S(2)}) collective-permute-start(f32[5,4,18,1]{3,2,1,0:T(8,128)S(1)} %get-tuple-element.11), channel_id=1, source_target_pairs={{1,0},{2,1},{3,2},{4,3},{5,4},{6,5},{7,6},{8,7},{9,8},{10,9},{11,1... | collective-permute-start | bytes 4328 | tf_op jit(solution)/shard_map/ppermute | solution.py:23
  328.8 12.8 %collective-permute-done.28 = f32[5,4,18,1]{3,2,1,0:T(8,128)S(1)} collective-permute-done((f32[5,4,18,1]{3,2,1,0:T(8,128)S(1)}, f32[5,4,18,1]{3,2,1,0:T(8,128)S(1)}, u32[]{:S(2)}, u32[]{:S(2)}) %collective-permute-start.28) | collective-permute-done | bytes 1472 | tf_op jit(solution)/shard_map/ppermute | solution.py:20
  347.4 20.0 %collective-permute-done.29 = f32[20,16,128]{2,1,0:T(8,128)S(1)} collective-permute-done((f32[20,16,128]{2,1,0:T(8,128)S(1)}, f32[20,16,128]{2,1,0:T(8,128)S(1)}, u32[]{:S(2)}, u32[]{:S(2)}) %collective-permute-start.29) | collective-permute-done | bytes 163872 | tf_op jit(solution)/shard_map/ppermute | solution.py:31
  369.4 19.7 %collective-permute-done.30 = f32[20,16,128]{2,1,0:T(8,128)S(1)} collective-permute-done((f32[20,16,128]{2,1,0:T(8,128)S(1)}, f32[20,16,128]{2,1,0:T(8,128)S(1)}, u32[]{:S(2)}, u32[]{:S(2)}) %collective-permute-start.30) | collective-permute-done | bytes 163872 | tf_op jit(solution)/shard_map/ppermute | solution.py:31
  391.1 6.8 %collective-permute-done.31 = f32[20,16,128]{2,1,0:T(8,128)S(1)} collective-permute-done((f32[20,16,128]{2,1,0:T(8,128)S(1)}, f32[20,16,128]{2,1,0:T(8,128)S(1)}, u32[]{:S(2)}, u32[]{:S(2)}) %collective-permute-start.31) | collective-permute-done | bytes 163872 | tf_op jit(solution)/shard_map/ppermute | solution.py:31
  400.3 6.4 %collective-permute-done.32 = f32[20,16,128]{2,1,0:T(8,128)S(1)} collective-permute-done((f32[20,16,128]{2,1,0:T(8,128)S(1)}, f32[20,16,128]{2,1,0:T(8,128)S(1)}, u32[]{:S(2)}, u32[]{:S(2)}) %collective-permute-start.32) | collective-permute-done | bytes 163872 | tf_op jit(solution)/shard_map/ppermute | solution.py:31
  408.9 17.0 %collective-permute-done.33 = f32[20,16,128]{2,1,0:T(8,128)S(1)} collective-permute-done((f32[20,16,128]{2,1,0:T(8,128)S(1)}, f32[20,16,128]{2,1,0:T(8,128)S(1)}, u32[]{:S(2)}, u32[]{:S(2)}) %collective-permute-start.33) | collective-permute-done | bytes 163872 | tf_op jit(solution)/shard_map/ppermute | solution.py:31
  (184 shorter events, 76.4 us)
Async XLA Ops:
  0.9 10.8 %collective-permute-start.1 = (f32[5,4,1,128]{3,2,1,0:T(1,128)S(1)}, f32[5,4,1,128]{3,2,1,0:T(1,128)S(1)}, u32[]{:S(2)}, u32[]{:S(2)}) collective-permute-start(f32[5,4,1,128]{3,2,1,0:T(1,128)S(1)} %get-tuple-element.44), channel_id=1, source_target_pairs={{0,16},{16,32},{32,48},{48,64},{64,80},{80,96},{96,112},{112,128},... | collective-permute-start | bytes 30728 | tf_op jit(solution)/shard_map/ppermute | solution.py:20
  2.9 8.9 %collective-permute-start = (f32[5,4,1,128]{3,2,1,0:T(1,128)S(1)}, f32[5,4,1,128]{3,2,1,0:T(1,128)S(1)}, u32[]{:S(2)}, u32[]{:S(2)}) collective-permute-start(f32[5,4,1,128]{3,2,1,0:T(1,128)S(1)} %get-tuple-element.45), channel_id=1, source_target_pairs={{16,0},{32,16},{48,32},{64,48},{80,64},{96,80},{112,96},{128,112},... | collective-permute-start | bytes 30728 | tf_op jit(solution)/shard_map/ppermute | solution.py:23
  12.0 24.9 %collective-permute-start.3 = (f32[5,4,18,1]{3,2,1,0:T(8,128)S(1)}, f32[5,4,18,1]{3,2,1,0:T(8,128)S(1)}, u32[]{:S(2)}, u32[]{:S(2)}) collective-permute-start(f32[5,4,18,1]{3,2,1,0:T(8,128)S(1)} %get-tuple-element.20), channel_id=1, source_target_pairs={{0,1},{1,2},{2,3},{3,4},{4,5},{5,6},{6,7},{7,8},{8,9},{9,10},{10,1... | collective-permute-start | bytes 4328 | tf_op jit(solution)/shard_map/ppermute | solution.py:20
  22.9 30.4 %collective-permute-start.2 = (f32[5,4,18,1]{3,2,1,0:T(8,128)S(1)}, f32[5,4,18,1]{3,2,1,0:T(8,128)S(1)}, u32[]{:S(2)}, u32[]{:S(2)}) collective-permute-start(f32[5,4,18,1]{3,2,1,0:T(8,128)S(1)} %get-tuple-element.21), channel_id=1, source_target_pairs={{1,0},{2,1},{3,2},{4,3},{5,4},{6,5},{7,6},{8,7},{9,8},{10,9},{11,1... | collective-permute-start | bytes 4328 | tf_op jit(solution)/shard_map/ppermute | solution.py:23
  54.1 8.4 %collective-permute-start.5 = (f32[5,4,1,128]{3,2,1,0:T(1,128)S(1)}, f32[5,4,1,128]{3,2,1,0:T(1,128)S(1)}, u32[]{:S(2)}, u32[]{:S(2)}) collective-permute-start(f32[5,4,1,128]{3,2,1,0:T(1,128)S(1)} %get-tuple-element.42), channel_id=1, source_target_pairs={{0,16},{16,32},{32,48},{48,64},{64,80},{80,96},{96,112},{112,128},... | collective-permute-start | bytes 30728 | tf_op jit(solution)/shard_map/ppermute | solution.py:20
  63.9 15.2 %collective-permute-start.7 = (f32[5,4,18,1]{3,2,1,0:T(8,128)S(1)}, f32[5,4,18,1]{3,2,1,0:T(8,128)S(1)}, u32[]{:S(2)}, u32[]{:S(2)}) collective-permute-start(f32[5,4,18,1]{3,2,1,0:T(8,128)S(1)} %get-tuple-element.18), channel_id=1, source_target_pairs={{0,1},{1,2},{2,3},{3,4},{4,5},{5,6},{6,7},{7,8},{8,9},{9,10},{10,1... | collective-permute-start | bytes 4328 | tf_op jit(solution)/shard_map/ppermute | solution.py:20
  70.7 15.8 %collective-permute-start.6 = (f32[5,4,18,1]{3,2,1,0:T(8,128)S(1)}, f32[5,4,18,1]{3,2,1,0:T(8,128)S(1)}, u32[]{:S(2)}, u32[]{:S(2)}) collective-permute-start(f32[5,4,18,1]{3,2,1,0:T(8,128)S(1)} %get-tuple-element.19), channel_id=1, source_target_pairs={{1,0},{2,1},{3,2},{4,3},{5,4},{6,5},{7,6},{8,7},{9,8},{10,9},{11,1... | collective-permute-start | bytes 4328 | tf_op jit(solution)/shard_map/ppermute | solution.py:23
  87.3 17.6 %collective-permute-start.9 = (f32[5,4,1,128]{3,2,1,0:T(1,128)S(1)}, f32[5,4,1,128]{3,2,1,0:T(1,128)S(1)}, u32[]{:S(2)}, u32[]{:S(2)}) collective-permute-start(f32[5,4,1,128]{3,2,1,0:T(1,128)S(1)} %get-tuple-element.40), channel_id=1, source_target_pairs={{0,16},{16,32},{32,48},{48,64},{64,80},{80,96},{96,112},{112,128},... | collective-permute-start | bytes 30728 | tf_op jit(solution)/shard_map/ppermute | solution.py:20
  89.3 16.9 %collective-permute-start.8 = (f32[5,4,1,128]{3,2,1,0:T(1,128)S(1)}, f32[5,4,1,128]{3,2,1,0:T(1,128)S(1)}, u32[]{:S(2)}, u32[]{:S(2)}) collective-permute-start(f32[5,4,1,128]{3,2,1,0:T(1,128)S(1)} %get-tuple-element.41), channel_id=1, source_target_pairs={{16,0},{32,16},{48,32},{64,48},{80,64},{96,80},{112,96},{128,112},... | collective-permute-start | bytes 30728 | tf_op jit(solution)/shard_map/ppermute | solution.py:23
  106.4 23.9 %collective-permute-start.11 = (f32[5,4,18,1]{3,2,1,0:T(8,128)S(1)}, f32[5,4,18,1]{3,2,1,0:T(8,128)S(1)}, u32[]{:S(2)}, u32[]{:S(2)}) collective-permute-start(f32[5,4,18,1]{3,2,1,0:T(8,128)S(1)} %get-tuple-element.16), channel_id=1, source_target_pairs={{0,1},{1,2},{2,3},{3,4},{4,5},{5,6},{6,7},{7,8},{8,9},{9,10},{10,1... | collective-permute-start | bytes 4328 | tf_op jit(solution)/shard_map/ppermute | solution.py:20
  110.1 24.2 %collective-permute-start.10 = (f32[5,4,18,1]{3,2,1,0:T(8,128)S(1)}, f32[5,4,18,1]{3,2,1,0:T(8,128)S(1)}, u32[]{:S(2)}, u32[]{:S(2)}) collective-permute-start(f32[5,4,18,1]{3,2,1,0:T(8,128)S(1)} %get-tuple-element.17), channel_id=1, source_target_pairs={{1,0},{2,1},{3,2},{4,3},{5,4},{6,5},{7,6},{8,7},{9,8},{10,9},{11,1... | collective-permute-start | bytes 4328 | tf_op jit(solution)/shard_map/ppermute | solution.py:23
  135.0 28.8 %collective-permute-start.12 = (f32[20,16,128]{2,1,0:T(8,128)S(1)}, f32[20,16,128]{2,1,0:T(8,128)S(1)}, u32[]{:S(2)}, u32[]{:S(2)}) collective-permute-start(f32[20,16,128]{2,1,0:T(8,128)S(1)} %bitcast.45), channel_id=1, source_target_pairs={{15,0},{0,1},{1,2},{2,3},{3,4},{4,5},{5,6},{6,7},{7,8},{8,9},{9,10... | collective-permute-start | bytes 491528 | tf_op jit(solution)/shard_map/ppermute | solution.py:31
  163.9 23.9 %collective-permute-start.13 = (f32[20,16,128]{2,1,0:T(8,128)S(1)}, f32[20,16,128]{2,1,0:T(8,128)S(1)}, u32[]{:S(2)}, u32[]{:S(2)}) collective-permute-start(f32[20,16,128]{2,1,0:T(8,128)S(1)} %broadcast_select_fusion.1), channel_id=1, source_target_pairs={{14,0},{15,1},{0,2},{1,3},{2,4},{3,5},{4,6},{5,7},{6,8},{7,9},{8,1... | collective-permute-start | bytes 491528 | tf_op jit(solution)/shard_map/ppermute | solution.py:31
  187.9 9.2 %collective-permute-start.14 = (f32[20,16,128]{2,1,0:T(8,128)S(1)}, f32[20,16,128]{2,1,0:T(8,128)S(1)}, u32[]{:S(2)}, u32[]{:S(2)}) collective-permute-start(f32[20,16,128]{2,1,0:T(8,128)S(1)} %broadcast_select_fusion.3), channel_id=1, source_target_pairs={{12,0},{13,1},{14,2},{15,3},{0,4},{1,5},{2,6},{3,7},{4,8},{5,9},{6... | collective-permute-start | bytes 491528 | tf_op jit(solution)/shard_map/ppermute | solution.py:31
  197.2 8.7 %collective-permute-start.15 = (f32[20,16,128]{2,1,0:T(8,128)S(1)}, f32[20,16,128]{2,1,0:T(8,128)S(1)}, u32[]{:S(2)}, u32[]{:S(2)}) collective-permute-start(f32[20,16,128]{2,1,0:T(8,128)S(1)} %broadcast_select_fusion.5), channel_id=1, source_target_pairs={{8,0},{9,1},{10,2},{11,3},{12,4},{13,5},{14,6},{15,7},{0,8},{1,9},... | collective-permute-start | bytes 491528 | tf_op jit(solution)/shard_map/ppermute | solution.py:31
  206.0 14.3 %collective-permute-start.16 = (f32[20,16,128]{2,1,0:T(8,128)S(1)}, f32[20,16,128]{2,1,0:T(8,128)S(1)}, u32[]{:S(2)}, u32[]{:S(2)}) collective-permute-start(f32[20,16,128]{2,1,0:T(8,128)S(1)} %broadcast_select_fusion.7), channel_id=1, source_target_pairs={{15,0},{0,1},{1,2},{2,3},{3,4},{4,5},{5,6},{6,7},{7,8},{8,9},{9,10... | collective-permute-start | bytes 491528 | tf_op jit(solution)/shard_map/ppermute | solution.py:31
  222.2 8.3 %collective-permute-start.18 = (f32[5,4,1,128]{3,2,1,0:T(1,128)S(1)}, f32[5,4,1,128]{3,2,1,0:T(1,128)S(1)}, u32[]{:S(2)}, u32[]{:S(2)}) collective-permute-start(f32[5,4,1,128]{3,2,1,0:T(1,128)S(1)} %get-tuple-element.38), channel_id=1, source_target_pairs={{0,16},{16,32},{32,48},{48,64},{64,80},{80,96},{96,112},{112,128},... | collective-permute-start | bytes 30728 | tf_op jit(solution)/shard_map/ppermute | solution.py:20
  232.0 22.7 %collective-permute-start.20 = (f32[5,4,18,1]{3,2,1,0:T(8,128)S(1)}, f32[5,4,18,1]{3,2,1,0:T(8,128)S(1)}, u32[]{:S(2)}, u32[]{:S(2)}) collective-permute-start(f32[5,4,18,1]{3,2,1,0:T(8,128)S(1)} %get-tuple-element.14), channel_id=1, source_target_pairs={{0,1},{1,2},{2,3},{3,4},{4,5},{5,6},{6,7},{7,8},{8,9},{9,10},{10,1... | collective-permute-start | bytes 4328 | tf_op jit(solution)/shard_map/ppermute | solution.py:20
  233.9 27.4 %collective-permute-start.19 = (f32[5,4,18,1]{3,2,1,0:T(8,128)S(1)}, f32[5,4,18,1]{3,2,1,0:T(8,128)S(1)}, u32[]{:S(2)}, u32[]{:S(2)}) collective-permute-start(f32[5,4,18,1]{3,2,1,0:T(8,128)S(1)} %get-tuple-element.15), channel_id=1, source_target_pairs={{1,0},{2,1},{3,2},{4,3},{5,4},{6,5},{7,6},{8,7},{9,8},{10,9},{11,1... | collective-permute-start | bytes 4328 | tf_op jit(solution)/shard_map/ppermute | solution.py:23
  262.1 11.6 %collective-permute-start.22 = (f32[5,4,1,128]{3,2,1,0:T(1,128)S(1)}, f32[5,4,1,128]{3,2,1,0:T(1,128)S(1)}, u32[]{:S(2)}, u32[]{:S(2)}) collective-permute-start(f32[5,4,1,128]{3,2,1,0:T(1,128)S(1)} %get-tuple-element.36), channel_id=1, source_target_pairs={{0,16},{16,32},{32,48},{48,64},{64,80},{80,96},{96,112},{112,128},... | collective-permute-start | bytes 30728 | tf_op jit(solution)/shard_map/ppermute | solution.py:20
  264.1 9.7 %collective-permute-start.21 = (f32[5,4,1,128]{3,2,1,0:T(1,128)S(1)}, f32[5,4,1,128]{3,2,1,0:T(1,128)S(1)}, u32[]{:S(2)}, u32[]{:S(2)}) collective-permute-start(f32[5,4,1,128]{3,2,1,0:T(1,128)S(1)} %get-tuple-element.37), channel_id=1, source_target_pairs={{16,0},{32,16},{48,32},{64,48},{80,64},{96,80},{112,96},{128,112},... | collective-permute-start | bytes 30728 | tf_op jit(solution)/shard_map/ppermute | solution.py:23
  274.0 26.5 %collective-permute-start.24 = (f32[5,4,18,1]{3,2,1,0:T(8,128)S(1)}, f32[5,4,18,1]{3,2,1,0:T(8,128)S(1)}, u32[]{:S(2)}, u32[]{:S(2)}) collective-permute-start(f32[5,4,18,1]{3,2,1,0:T(8,128)S(1)} %get-tuple-element.12), channel_id=1, source_target_pairs={{0,1},{1,2},{2,3},{3,4},{4,5},{5,6},{6,7},{7,8},{8,9},{9,10},{10,1... | collective-permute-start | bytes 4328 | tf_op jit(solution)/shard_map/ppermute | solution.py:20
  276.4 24.1 %collective-permute-start.23 = (f32[5,4,18,1]{3,2,1,0:T(8,128)S(1)}, f32[5,4,18,1]{3,2,1,0:T(8,128)S(1)}, u32[]{:S(2)}, u32[]{:S(2)}) collective-permute-start(f32[5,4,18,1]{3,2,1,0:T(8,128)S(1)} %get-tuple-element.13), channel_id=1, source_target_pairs={{1,0},{2,1},{3,2},{4,3},{5,4},{6,5},{7,6},{8,7},{9,8},{10,9},{11,1... | collective-permute-start | bytes 4328 | tf_op jit(solution)/shard_map/ppermute | solution.py:23
  301.3 15.4 %collective-permute-start.26 = (f32[5,4,1,128]{3,2,1,0:T(1,128)S(1)}, f32[5,4,1,128]{3,2,1,0:T(1,128)S(1)}, u32[]{:S(2)}, u32[]{:S(2)}) collective-permute-start(f32[5,4,1,128]{3,2,1,0:T(1,128)S(1)} %get-tuple-element.34), channel_id=1, source_target_pairs={{0,16},{16,32},{32,48},{48,64},{64,80},{80,96},{96,112},{112,128},... | collective-permute-start | bytes 30728 | tf_op jit(solution)/shard_map/ppermute | solution.py:20
  303.2 13.4 %collective-permute-start.25 = (f32[5,4,1,128]{3,2,1,0:T(1,128)S(1)}, f32[5,4,1,128]{3,2,1,0:T(1,128)S(1)}, u32[]{:S(2)}, u32[]{:S(2)}) collective-permute-start(f32[5,4,1,128]{3,2,1,0:T(1,128)S(1)} %get-tuple-element.35), channel_id=1, source_target_pairs={{16,0},{32,16},{48,32},{64,48},{80,64},{96,80},{112,96},{128,112},... | collective-permute-start | bytes 30728 | tf_op jit(solution)/shard_map/ppermute | solution.py:23
  316.9 24.7 %collective-permute-start.28 = (f32[5,4,18,1]{3,2,1,0:T(8,128)S(1)}, f32[5,4,18,1]{3,2,1,0:T(8,128)S(1)}, u32[]{:S(2)}, u32[]{:S(2)}) collective-permute-start(f32[5,4,18,1]{3,2,1,0:T(8,128)S(1)} %get-tuple-element.10), channel_id=1, source_target_pairs={{0,1},{1,2},{2,3},{3,4},{4,5},{5,6},{6,7},{7,8},{8,9},{9,10},{10,1... | collective-permute-start | bytes 4328 | tf_op jit(solution)/shard_map/ppermute | solution.py:20
  319.7 25.0 %collective-permute-start.27 = (f32[5,4,18,1]{3,2,1,0:T(8,128)S(1)}, f32[5,4,18,1]{3,2,1,0:T(8,128)S(1)}, u32[]{:S(2)}, u32[]{:S(2)}) collective-permute-start(f32[5,4,18,1]{3,2,1,0:T(8,128)S(1)} %get-tuple-element.11), channel_id=1, source_target_pairs={{1,0},{2,1},{3,2},{4,3},{5,4},{6,5},{7,6},{8,7},{9,8},{10,9},{11,1... | collective-permute-start | bytes 4328 | tf_op jit(solution)/shard_map/ppermute | solution.py:23
  345.5 21.9 %collective-permute-start.29 = (f32[20,16,128]{2,1,0:T(8,128)S(1)}, f32[20,16,128]{2,1,0:T(8,128)S(1)}, u32[]{:S(2)}, u32[]{:S(2)}) collective-permute-start(f32[20,16,128]{2,1,0:T(8,128)S(1)} %bitcast.46), channel_id=1, source_target_pairs={{15,0},{0,1},{1,2},{2,3},{3,4},{4,5},{5,6},{6,7},{7,8},{8,9},{9,10... | collective-permute-start | bytes 491528 | tf_op jit(solution)/shard_map/ppermute | solution.py:31
  367.4 21.7 %collective-permute-start.30 = (f32[20,16,128]{2,1,0:T(8,128)S(1)}, f32[20,16,128]{2,1,0:T(8,128)S(1)}, u32[]{:S(2)}, u32[]{:S(2)}) collective-permute-start(f32[20,16,128]{2,1,0:T(8,128)S(1)} %broadcast_select_fusion), channel_id=1, source_target_pairs={{14,0},{15,1},{0,2},{1,3},{2,4},{3,5},{4,6},{5,7},{6,8},{7,9},{8,1... | collective-permute-start | bytes 491528 | tf_op jit(solution)/shard_map/ppermute | solution.py:31
  389.2 8.8 %collective-permute-start.31 = (f32[20,16,128]{2,1,0:T(8,128)S(1)}, f32[20,16,128]{2,1,0:T(8,128)S(1)}, u32[]{:S(2)}, u32[]{:S(2)}) collective-permute-start(f32[20,16,128]{2,1,0:T(8,128)S(1)} %broadcast_select_fusion.2), channel_id=1, source_target_pairs={{12,0},{13,1},{14,2},{15,3},{0,4},{1,5},{2,6},{3,7},{4,8},{5,9},{6... | collective-permute-start | bytes 491528 | tf_op jit(solution)/shard_map/ppermute | solution.py:31
  398.1 8.7 %collective-permute-start.32 = (f32[20,16,128]{2,1,0:T(8,128)S(1)}, f32[20,16,128]{2,1,0:T(8,128)S(1)}, u32[]{:S(2)}, u32[]{:S(2)}) collective-permute-start(f32[20,16,128]{2,1,0:T(8,128)S(1)} %broadcast_select_fusion.4), channel_id=1, source_target_pairs={{8,0},{9,1},{10,2},{11,3},{12,4},{13,5},{14,6},{15,7},{0,8},{1,9},... | collective-permute-start | bytes 491528 | tf_op jit(solution)/shard_map/ppermute | solution.py:31
  406.9 19.1 %collective-permute-start.33 = (f32[20,16,128]{2,1,0:T(8,128)S(1)}, f32[20,16,128]{2,1,0:T(8,128)S(1)}, u32[]{:S(2)}, u32[]{:S(2)}) collective-permute-start(f32[20,16,128]{2,1,0:T(8,128)S(1)} %broadcast_select_fusion.6), channel_id=1, source_target_pairs={{15,0},{0,1},{1,2},{2,3},{3,4},{4,5},{5,6},{6,7},{7,8},{8,9},{9,10... | collective-permute-start | bytes 491528 | tf_op jit(solution)/shard_map/ppermute | solution.py:31
  (20 other events, 279.8 us)
where the time goes:
time: 430 us; the launch traced here: 428 us
  waiting for transfers between devices  253 us (59%)
  starting transfers between devices  161 us (37%)
  other arithmetic  8.76 us (2%)
  local copies, waits for them, and re-layouts  4.79 us (1%)
    ppermute x10, waiting for transfers between devices, from_behind(): return lax.ppermute(block, axis, route)  145 us
    ppermute x12, starting transfers between devices, extended_2(): lax.ppermute(lax.slice_in_dim(block, 0, width, axis=dim), axis, backward)  101 us
    ppermute x12, waiting for transfers between devices, extended_2(): lax.ppermute(lax.slice_in_dim(block, block.shape[dim] - width, None, axis...  66.8 us
    ppermute x12, waiting for transfers between devices, extended_2(): lax.ppermute(lax.slice_in_dim(block, 0, width, axis=dim), axis, backward)  41.4 us
    ppermute x12, starting transfers between devices, extended_2(): lax.ppermute(lax.slice_in_dim(block, block.shape[dim] - width, None, axis...  40 us
    ppermute x10, starting transfers between devices, from_behind(): return lax.ppermute(block, axis, route)  20 us
  transfers between devices with their start and end apart: 34, of which 26 were waited for; matrix products, arithmetic and copies ran while one was open for 0% of the time, Pallas kernels for 0%

commit v1 on v0

v1 whole, which is shorter than its diff:
```python
import jax
import jax.numpy as jnp
from jax import lax
from jax.experimental import pallas as pl
from jax.experimental.pallas import tpu as pltpu
from jax.sharding import PartitionSpec as P

STEPS = 2
DT = 0.15
HD = 0.5 * DT
NEAR = DT * 0.05
SELF = 4.0 * DT * 0.05

FIELDS = 5
LEVELS = 4
PLANES = FIELDS * LEVELS
ROWS = 16
LANES = 128
REACH = 3
HALO = 2 * REACH
TALL = 32
PACK = 24


def put_together(main, below, above, all_ref, edge_ref):
    lane = lax.broadcasted_iota(jnp.int32, (TALL, LANES), 1)
    edge = jnp.zeros((TALL, LANES), jnp.float32)
    for plane in range(PLANES):
        f, k = divmod(plane, LEVELS)
        all_ref[plane, 0:ROWS, :] = main[f, k]
        all_ref[plane, ROWS : ROWS + HALO, :] = below[f, k]
        all_ref[plane, ROWS + HALO : TALL - HALO, :] = jnp.zeros(
            (TALL - ROWS - 2 * HALO, LANES), jnp.float32
        )
        all_ref[plane, TALL - HALO : TALL, :] = above[f, k]
    for plane in range(PLANES):
        cells = all_ref[plane]
        if plane:
            cells = pltpu.roll(cells, HALO * plane, 1)
        here = (lane >= HALO * plane) & (lane < HALO * (plane + 1))
        edge = jnp.where(here, cells, edge)
    edge_ref[...] = edge


def advance(at, slopes, coefs):
    a1, a2, twice, half, stiff = coefs
    rho, u, v, w, p = [slopes(f) for f in range(FIELDS)]
    w_up, w_down, p_up, p_down = at
    g = (u[1] - u[2]) + (v[3] - v[4])
    if w_up is not None:
        g = g + w_up
    if w_down is not None:
        g = g - w_down
    g = HD * g
    lift = 0.0
    if p_up is not None:
        lift = lift + p_up
    if p_down is not None:
        lift = lift - p_down
    own = [
        -g,
        twice * v[0] - HD * (p[1] - p[2]),
        -(half * u[0]) - HD * (p[3] - p[4]),
        -HD * lift,
        -(stiff * g),
    ]
    return [
        extra + ((a1 * q[3] + a2 * q[4]) + (NEAR * (q[1] + q[2]) - SELF * q[0]))
        for extra, q in zip(own, (rho, u, v, w, p))
    ]


def combine(stage, start, now, change):
    if stage == 0:
        return now + change
    if stage == 1:
        return 0.75 * start + 0.25 * (now + change)
    return start * (1.0 / 3.0) + (2.0 / 3.0) * (now + change)


def first_step(all_ref, edge_ref, coef_ref, send_ref, begin, one, two, table):
    wide = 2 * LANES
    edge = edge_ref[...]
    for plane in range(PLANES):
        begin[plane, :, 0:LANES] = all_ref[plane]
        begin[plane, :, LANES:wide] = (
            pltpu.roll(edge, LANES - HALO * plane, 1) if plane else edge
        )

    def coef(i):
        part = coef_ref[i]
        return jnp.concatenate([part, part], axis=1)

    sources = (begin, one, two)
    targets = (one, two, None)
    lane = lax.broadcasted_iota(jnp.int32, (TALL, LANES), 1)
    for stage in range(3):
        src, dst = sources[stage], targets[stage]
        for k in range(LEVELS):

            def slopes(f):
                c = src[f * LEVELS + k]
                return (
                    c,
                    pltpu.roll(c, TALL - 1, 0),
                    pltpu.roll(c, 1, 0),
                    pltpu.roll(c, wide - 1, 1),
                    pltpu.roll(c, 1, 1),
                )

            at = (
                src[3 * LEVELS + k + 1] if k + 1 < LEVELS else None,
                src[3 * LEVELS + k - 1] if k else None,
                src[4 * LEVELS + k + 1] if k + 1 < LEVELS else None,
                src[4 * LEVELS + k - 1] if k else None,
            )
            coefs = (coef(0), coef(1), coef(2), coef(3), coef(4 + k))
            valid = coef(4 + LEVELS) > 0.5
            change = advance(at, slopes, coefs)
            for f in range(FIELDS):
                plane = f * LEVELS + k
                value = combine(stage, begin[plane], src[plane], change[f])
                value = jnp.where(valid, value, 0.0)
                if dst is not None:
                    dst[plane] = value
                else:
                    left = pltpu.roll(value[:, 0:LANES], LANES - REACH, 1)
                    right = pltpu.roll(value[:, LANES:wide], LANES - REACH, 1)
                    shown = jnp.where(lane < LANES - REACH, left, right)
                    shown = pltpu.roll(shown, REACH, 0)
                    table[pl.ds(plane, PACK, PLANES), :] = shown[0:PACK]
    size = (4 + HALO) * PLANES
    for group in range(4):
        send_ref[group] = table[group * 4 * PLANES : group * 4 * PLANES + size]


def spread(got_ref, send_ref):
    size = (1 + HALO) * PLANES
    for target in range(4):
        for z in range(4):
            send_ref[target, z] = got_ref[z, target * PLANES : target * PLANES + size]


def turned(cells, amount, lane):
    blocks = amount // LANES
    offset = amount % LANES
    cells = pltpu.roll(cells, offset, 1)
    near = pltpu.roll(cells, blocks, 0)
    far = pltpu.roll(cells, lax.rem(blocks + 1, 16), 0)
    return jnp.where(lane >= offset, near, far)


def second_step(amount_ref, coef_ref, got_ref, send_ref, begin, one, two):
    lane = lax.broadcasted_iota(jnp.int32, (16, LANES), 1)
    span = 1 + HALO
    for row in range(span):
        amount = amount_ref[row]
        for plane in range(PLANES):
            cells = got_ref[pl.ds(row * PLANES + plane, 16, span * PLANES), :]
            begin[row, plane] = turned(cells, amount, lane)

    sources = (begin, one, two)
    targets = (one, two, None)
    last_amount = amount_ref[span]
    for stage in range(3):
        src, dst = sources[stage], targets[stage]
        for row in range(stage + 1, span - 1 - stage):
            scalars = [coef_ref[row, i] for i in range(5 + LEVELS)]
            for k in range(LEVELS):

                def slopes(f):
                    plane = f * LEVELS + k
                    c = src[row, plane]
                    ahead = pltpu.roll(c, LANES - 1, 1)
                    ahead = jnp.where(
                        lane == LANES - 1, pltpu.roll(ahead, 15, 0), ahead
                    )
                    behind = pltpu.roll(c, 1, 1)
                    behind = jnp.where(lane == 0, pltpu.roll(behind, 1, 0), behind)
                    return c, src[row + 1, plane], src[row - 1, plane], ahead, behind

                at = (
                    src[row, 3 * LEVELS + k + 1] if k + 1 < LEVELS else None,
                    src[row, 3 * LEVELS + k - 1] if k else None,
                    src[row, 4 * LEVELS + k + 1] if k + 1 < LEVELS else None,
                    src[row, 4 * LEVELS + k - 1] if k else None,
                )
                coefs = tuple(scalars[0:4]) + (scalars[4 + k],)
                change = advance(at, slopes, coefs)
                for f in range(FIELDS):
                    plane = f * LEVELS + k
                    value = combine(stage, begin[row, plane], src[row, plane], change[f])
                    if row != REACH:
                        value = jnp.where(scalars[4 + LEVELS] > 0.5, value, 0.0)
                    if dst is not None:
                        dst[row, plane] = value
                    else:
                        send_ref[pl.ds(plane, 16, PACK), :] = turned(
                            value, last_amount, lane
                        )
    for j in range(16):
        send_ref[j * PACK + PLANES : (j + 1) * PACK, :] = jnp.zeros(
            (PACK - PLANES, LANES), jnp.float32
        )


def set_down(got_ref, out_ref):
    for plane in range(PLANES):
        f, k = divmod(plane, LEVELS)
        for z in range(4):
            out_ref[f, k, 4 * z : 4 * z + 4, :] = got_ref[
                pl.ds(z * PACK + plane, 4, 4 * PACK), :
            ]


VMEM = pl.BlockSpec(memory_space=pltpu.VMEM)
SMEM = pl.BlockSpec(memory_space=pltpu.SMEM)


def f32(*shape):
    return jax.ShapeDtypeStruct(shape, jnp.float32)


def call(body, out_shape, in_specs, scratch=()):
    many = isinstance(out_shape, tuple)
    return pl.pallas_call(
        body,
        name=body.__name__,
        out_shape=out_shape,
        in_specs=in_specs,
        out_specs=(VMEM,) * len(out_shape) if many else VMEM,
        scratch_shapes=list(scratch),
    )


def on_device(state, shifts, spin, drift, stiffness):
    rad = lax.axis_size("rad")
    azi = lax.axis_size("azi")
    ring = lax.axis_index("azi")
    total = spin.shape[0]
    row_start = lax.axis_index("rad") * ROWS

    below = lax.ppermute(
        state[:, :, 0:HALO, :], "rad", [(i + 1, i) for i in range(rad - 1)]
    )
    above = lax.ppermute(
        state[:, :, ROWS - HALO :, :], "rad", [(i, i + 1) for i in range(rad - 1)]
    )

    rows = jnp.concatenate(
        [
            jnp.stack(
                [
                    NEAR - HD * drift,
                    NEAR + HD * drift,
                    (2.0 * DT) * spin,
                    (0.5 * DT) * spin,
                ]
            ),
            stiffness,
            jnp.ones((1, total), jnp.float32),
        ],
        axis=0,
    )
    rows = jnp.pad(rows, ((0, 0), (HALO, HALO)))
    near = lax.dynamic_slice_in_dim(rows, row_start, ROWS + 2 * HALO, axis=1)
    near = jnp.concatenate(
        [
            near[:, HALO:],
            jnp.zeros((rows.shape[0], TALL - ROWS - 2 * HALO), jnp.float32),
            near[:, :HALO],
        ],
        axis=1,
    )
    near = jnp.broadcast_to(near[:, :, None], near.shape + (LANES,))

    own_row = row_start + 4 * (ring % 4) + ring // 4
    around = lax.dynamic_slice_in_dim(rows, own_row + REACH, 1 + HALO, axis=1).T
    turn = lax.dynamic_slice_in_dim(
        jnp.pad(shifts, (REACH, REACH)), own_row, 1 + HALO, axis=0
    )
    turn = jnp.concatenate([(turn + REACH) % (azi * LANES), turn[REACH : REACH + 1]])

    whole, edge = call(
        put_together, (f32(PLANES, TALL, LANES), f32(TALL, LANES)), [VMEM] * 3
    )(state, below, above)
    edge = lax.ppermute(edge, "azi", [((i + 1) % azi, i) for i in range(azi)])

    count = (4 + HALO) * PLANES
    tile = pltpu.VMEM((PLANES, TALL, 2 * LANES), jnp.float32)
    sent = call(
        first_step,
        f32(4, count, LANES),
        [VMEM] * 3,
        (tile, tile, tile, pltpu.VMEM((PACK * PLANES, LANES), jnp.float32)),
    )(whole, edge, near)
    along_z = [[4 * x + z for z in range(4)] for x in range(4)]
    along_x = [[4 * x + z for x in range(4)] for z in range(4)]
    got = lax.all_to_all(sent, "azi", 0, 0, axis_index_groups=along_z)
    size = (1 + HALO) * PLANES
    sent = call(spread, f32(4, 4, size, LANES), [VMEM])(got)
    got = lax.all_to_all(
        sent.reshape(4, 4 * size, LANES), "azi", 0, 0, axis_index_groups=along_x
    )
    band = pltpu.VMEM((1 + HALO, PLANES, 16, LANES), jnp.float32)
    sent = call(
        second_step, f32(16 * PACK, LANES), [SMEM, SMEM, VMEM], (band, band, band)
    )(turn, around, got.reshape(16 * size, LANES))
    got = lax.all_to_all(sent.reshape(16, PACK, LANES), "azi", 0, 0)
    return call(set_down, f32(FIELDS, LEVELS, ROWS, LANES), [VMEM])(
        got.reshape(16 * PACK, LANES)
    )


def solution(mesh):
    in_specs = (P(None, None, "rad", "azi"), P(), P(), P(), P())
    out_specs = P(None, None, "rad", "azi")
    return jax.shard_map(
        on_device, mesh=mesh, in_specs=in_specs, out_specs=out_specs, check_vma=False
    )
```

time: 430 us -> 124 us (0.29)
  the two profiles are of different devices: /device:TPU:8 before, /device:TPU:120 now
where the time goes in v1:
time: 124 us
  blocking collectives  53.8 us (43%)
  starting transfers between devices  30.1 us (24%)
  waiting for transfers between devices  15.2 us (12%)
  Pallas kernels  12.8 us (10%)
  local copies, waits for them, and re-layouts  8.69 us (7%)
  other arithmetic  2.77 us (2%)
    all_to_all x1, blocking collectives, on_device(): got = lax.all_to_all(sent, 'azi', 0, 0, axis_index_groups=along_z)  33.1 us
    all_to_all x1, blocking collectives, on_device(): got = lax.all_to_all(sent.reshape(16, PACK, LANES), 'azi', 0, 0)  20.8 us
    ppermute x1, starting transfers between devices, on_device(): edge = lax.ppermute(edge, 'azi', [((i + 1) % azi, i) for i in range(azi)])  19.5 us
    all_to_all x1, waiting for transfers between devices, on_device(): lax.all_to_all(sent.reshape(4, 4 * size, LANES), 'azi', 0, 0, axis_index_...  13.8 us
    all_to_all x1, starting transfers between devices, on_device(): lax.all_to_all(sent.reshape(4, 4 * size, LANES), 'azi', 0, 0, axis_index_...  5.1 us
    pallas_call x1, Pallas kernels, on_device(): call(first_step, f32(4, count, LANES), [VMEM] * 3, (tile, tile, tile, plt...  3.69 us
    ppermute x1, starting transfers between devices, on_device(): lax.ppermute(state[:, :, 0:HALO, :], 'rad', [(i + 1, i) for i in range(ra...  3.64 us
    pallas_call x1, Pallas kernels, on_device(): call(second_step, f32(16 * PACK, LANES), [SMEM, SMEM, VMEM], (band, band,...  3.47 us
  transfers between devices with their start and end apart: 4, of which 2 were waited for; matrix products, arithmetic and copies ran while one was open for 4% of the time, Pallas kernels for 0%

profile of v1, /device:TPU:120, one launch (start us, length us, event | category | flops | bytes accessed | tf_op | source)
XLA Modules:
  0.0 123.5 jit_solution(9207629310228430809)
XLA Ops:
  0.0 0.9 fusion.2
  0.9 1.9 %collective-permute-start.1 = (f32[5,4,6,128]{3,2,1,0:T(8,128)S(1)}, f32[5,4,6,128]{3,2,1,0:T(8,128)S(1)}, u32[]{:S(2)}, u32[]{:S(2)}) collective-permute-start(f32[5,4,6,128]{3,2,1,0:T(8,128)S(1)} %get-tuple-element.11), channel_id=1, source_target_pairs={{0,16},{16,32},{32,48},{48,64},{64,80},{80,96},{96,112},{112,128},... | collective-permute-start | bytes 184328 | tf_op jit(solution)/shard_map/ppermute | solution.py:246
  2.9 3.6 %collective-permute-start = (f32[5,4,6,128]{3,2,1,0:T(8,128)S(1)}, f32[5,4,6,128]{3,2,1,0:T(8,128)S(1)}, u32[]{:S(2)}, u32[]{:S(2)}) collective-permute-start(f32[5,4,6,128]{3,2,1,0:T(8,128)S(1)} %get-tuple-element.12), channel_id=1, source_target_pairs={{16,0},{32,16},{48,32},{64,48},{80,64},{96,80},{112,96},{128,112},... | collective-permute-start | bytes 184328 | tf_op jit(solution)/shard_map/ppermute | solution.py:243
  6.5 0.7 broadcast_multiply_fusion.1
  7.2 0.7 multiply_add_fusion
  7.9 0.8 concatenate.10
  8.7 0.2 copy.14
  8.9 0.1 pad.11.clone
  9.0 0.0 collective-permute-done.1.above
  9.1 0.0 collective-permute-done.below
  9.1 0.6 copy-done.1
  9.7 0.6 copy-done.2
  10.3 1.8 %put_together.1 = (f32[20,32,128]{2,1,0:T(8,128)}, f32[32,128]{1,0:T(8,128)}) custom-call(f32[5,4,16,128]{3,2,1,0:T(8,128)} %main.1, f32[5,4,6,128]{3,2,1,0:T(8,128)} %copy-done.2, f32[5,4,6,128]{3,2,1,0:T(8,128)} %copy-done.1), custom_call_target="tpu_custom_call" | custom-call | tf_op jit(solution)/shard_map/put_together/pallas_call | solution.py:284
  12.1 19.5 %collective-permute-start.2 = (f32[32,128]{1,0:T(8,128)}, f32[32,128]{1,0:T(8,128)S(1)}, u32[]{:S(2)}, u32[]{:S(2)}) collective-permute-start(f32[32,128]{1,0:T(8,128)} %get-tuple-element.8), channel_id=1, source_target_pairs={{1,0},{2,1},{3,2},{4,3},{5,4},{6,5},{7,6},{8,7},{9,8},{10,9},{11,1... | collective-permute-start | bytes 49160 | tf_op jit(solution)/shard_map/ppermute | solution.py:287
  31.6 0.1 pad_maximum_fusion
  31.6 0.1 copy.15
  31.7 1.5 %collective-permute-done.2.edge_ref = f32[32,128]{1,0:T(8,128)S(1)} collective-permute-done((f32[32,128]{1,0:T(8,128)}, f32[32,128]{1,0:T(8,128)S(1)}, u32[]{:S(2)}, u32[]{:S(2)}) %collective-permute-start.2) | collective-permute-done | bytes 16416 | tf_op jit(solution)/shard_map/ppermute | solution.py:287
  33.2 0.8 broadcast_in_dim.14.coef_ref
  34.0 3.7 %first_step.1 = f32[4,200,128]{2,1,0:T(8,128)} custom-call(f32[20,32,128]{2,1,0:T(8,128)} %get-tuple-element.7.all_ref, f32[32,128]{1,0:T(8,128)} %copy-done.3, f32[9,32,128]{2,1,0:T(8,128)} %broadcast_in_dim.14.coef_ref), custom_call_target="tpu_custom_call" | custom-call | tf_op jit(solution)/shard_map/first_step/pallas_call | solution.py:291
  37.7 33.1 %all_to_all.15.got_ref = f32[4,200,128]{2,1,0:T(8,128)} all-to-all(f32[4,200,128]{2,1,0:T(8,128)} %first_step.1), channel_id=1, replica_groups={{0,1,2,3},{4,5,6,7},{8,9,10,11},{12,13,14,15},{16,17,18,19},{20,21,22,2..., dimensions={0} | all-to-all | bytes 819200 | tf_op jit(solution)/shard_map/all_to_all | solution.py:299
  70.7 2.1 %spread.1 = f32[4,4,140,128]{3,2,1,0:T(8,128)} custom-call(f32[4,200,128]{2,1,0:T(8,128)} %all_to_all.15.got_ref), custom_call_target="tpu_custom_call" | custom-call | tf_op jit(solution)/shard_map/spread/pallas_call | solution.py:301
  72.8 2.3 %reshape.13 = f32[4,560,128]{2,1,0:T(8,128)} reshape(f32[4,4,140,128]{3,2,1,0:T(8,128)} %spread.1) | data formatting | bytes 2293760 | tf_op jit(solution)/shard_map/reshape | solution.py:303
  75.2 5.1 %all-to-all-start.1 = ((f32[4,560,128]{2,1,0:T(8,128)}), f32[4,560,128]{2,1,0:T(8,128)S(1)}, u32[]{:S(2)}, u32[]{:S(2)}) async-start(f32[4,560,128]{2,1,0:T(8,128)} %reshape.13), calls=%async_computation.1 | async-start | bytes 2293760 | tf_op jit(solution)/shard_map/all_to_all | solution.py:302
  80.3 0.1 and_select_fusion
  80.4 0.6 slice.15
  81.0 1.2 pad_add_fusion.amount_ref
  82.2 0.6 fusion.coef_ref
  82.8 13.8 %all-to-all-done.1 = f32[4,560,128]{2,1,0:T(8,128)S(1)} async-done(((f32[4,560,128]{2,1,0:T(8,128)}), f32[4,560,128]{2,1,0:T(8,128)S(1)}, u32[]{:S(2)}, u32[]{:S(2)}) %all-to-all-start.1) | async-done | bytes 1146912 | tf_op jit(solution)/shard_map/all_to_all | solution.py:302
  96.6 1.0 copy-done
  97.6 3.5 %second_step.1 = f32[384,128]{1,0:T(8,128)} custom-call(s32[8]{0:T(128)} %pad_add_fusion.amount_ref, f32[7,9]{1,0:T(8,128)} %fusion.coef_ref, f32[2240,128]{1,0:T(8,128)} %bitcast.9), custom_call_target="tpu_custom_call" | custom-call | tf_op jit(solution)/shard_map/second_step/pallas_call | solution.py:306
  101.1 20.8 %all_to_all.16 = f32[16,24,128]{2,1,0:T(8,128)} all-to-all(f32[16,24,128]{2,1,0:T(8,128)} %bitcast.10), channel_id=1, replica_groups=mesh['rad'=64,'azi'=16] {'azi'}, dimensions={0} | all-to-all | bytes 393216 | tf_op jit(solution)/shard_map/all_to_all | solution.py:309
  121.8 1.7 %set_down.1 = f32[5,4,16,128]{3,2,1,0:T(8,128)} custom-call(f32[384,128]{1,0:T(8,128)} %bitcast.11), custom_call_target="tpu_custom_call" | custom-call | tf_op jit(solution)/shard_map/set_down/pallas_call | solution.py:310
  (11 shorter events, 0.0 us)
Async XLA Ops:
  0.9 8.1 %collective-permute-start.1 = (f32[5,4,6,128]{3,2,1,0:T(8,128)S(1)}, f32[5,4,6,128]{3,2,1,0:T(8,128)S(1)}, u32[]{:S(2)}, u32[]{:S(2)}) collective-permute-start(f32[5,4,6,128]{3,2,1,0:T(8,128)S(1)} %get-tuple-element.11), channel_id=1, source_target_pairs={{0,16},{16,32},{32,48},{48,64},{64,80},{80,96},{96,112},{112,128},... | collective-permute-start | bytes 184328 | tf_op jit(solution)/shard_map/ppermute | solution.py:246
  2.9 6.2 %collective-permute-start = (f32[5,4,6,128]{3,2,1,0:T(8,128)S(1)}, f32[5,4,6,128]{3,2,1,0:T(8,128)S(1)}, u32[]{:S(2)}, u32[]{:S(2)}) collective-permute-start(f32[5,4,6,128]{3,2,1,0:T(8,128)S(1)} %get-tuple-element.12), channel_id=1, source_target_pairs={{16,0},{32,16},{48,32},{64,48},{80,64},{96,80},{112,96},{128,112},... | collective-permute-start | bytes 184328 | tf_op jit(solution)/shard_map/ppermute | solution.py:243
  9.0 0.6 copy-start.1
  9.7 0.6 copy-start.2
  12.1 21.1 %collective-permute-start.2 = (f32[32,128]{1,0:T(8,128)}, f32[32,128]{1,0:T(8,128)S(1)}, u32[]{:S(2)}, u32[]{:S(2)}) collective-permute-start(f32[32,128]{1,0:T(8,128)} %get-tuple-element.8), channel_id=1, source_target_pairs={{1,0},{2,1},{3,2},{4,3},{5,4},{6,5},{7,6},{8,7},{9,8},{10,9},{11,1... | collective-permute-start | bytes 49160 | tf_op jit(solution)/shard_map/ppermute | solution.py:287
  33.2 0.8 copy-start.3
  75.2 5.1 %copy-start.4 = (s32[1024]{0:T(1024)S(1)}, s32[1024]{0:T(1024)}, u32[]{:S(2)}) copy-start(s32[1024]{0:T(1024)} %param.6) | copy-start | bytes 12292
  75.2 21.4 %all-to-all-start.1 = ((f32[4,560,128]{2,1,0:T(8,128)}), f32[4,560,128]{2,1,0:T(8,128)S(1)}, u32[]{:S(2)}, u32[]{:S(2)}) async-start(f32[4,560,128]{2,1,0:T(8,128)} %reshape.13), calls=%async_computation.1 | async-start | bytes 2293760 | tf_op jit(solution)/shard_map/all_to_all | solution.py:302
  96.6 1.0 copy-start

commit v2 on v1

--- a/solution.py
+++ b/solution.py
@@ -20,6 +20,7 @@
 HALO = 2 * REACH
 TALL = 32
 PACK = 24
+ROOM = 16 * 1024 * 1024
 
 
 def put_together(main, below, above, all_ref, edge_ref):
@@ -78,7 +79,7 @@
     return start * (1.0 / 3.0) + (2.0 / 3.0) * (now + change)
 
 
-def first_step(all_ref, edge_ref, coef_ref, send_ref, begin, one, two, table):
+def first_step(all_ref, edge_ref, row_ref, send_ref, begin, one, two, table, coef_ref):
     wide = 2 * LANES
     edge = edge_ref[...]
     for plane in range(PLANES):
@@ -86,6 +87,9 @@
         begin[plane, :, LANES:wide] = (
             pltpu.roll(edge, LANES - HALO * plane, 1) if plane else edge
         )
+
+    for i in range(coef_ref.shape[0]):
+        coef_ref[i] = jnp.broadcast_to(row_ref[:, i : i + 1], (TALL, LANES))
 
     def coef(i):
         part = coef_ref[i]
@@ -138,7 +142,9 @@
     size = (1 + HALO) * PLANES
     for target in range(4):
         for z in range(4):
-            send_ref[target, z] = got_ref[z, target * PLANES : target * PLANES + size]
+            send_ref[target, z * size : (z + 1) * size, :] = got_ref[
+                z, target * PLANES : target * PLANES + size, :
+            ]
 
 
 def turned(cells, amount, lane):
@@ -230,6 +236,7 @@
         in_specs=in_specs,
         out_specs=(VMEM,) * len(out_shape) if many else VMEM,
         scratch_shapes=list(scratch),
+        compiler_params=pltpu.CompilerParams(vmem_limit_bytes=ROOM),
     )
 
 
@@ -246,6 +253,14 @@
     above = lax.ppermute(
         state[:, :, ROWS - HALO :, :], "rad", [(i, i + 1) for i in range(rad - 1)]
     )
+
+    whole, edge = call(
+        put_together, (f32(PLANES, TALL, LANES), f32(TALL, LANES)), [VMEM] * 3
+    )(state, below, above)
+    spin, drift, stiffness, shifts, edge = lax.optimization_barrier(
+        (spin, drift, stiffness, shifts, edge)
+    )
+    edge = lax.ppermute(edge, "azi", [((i + 1) % azi, i) for i in range(azi)])
 
     rows = jnp.concatenate(
         [
@@ -272,7 +287,7 @@
         ],
         axis=1,
     )
-    near = jnp.broadcast_to(near[:, :, None], near.shape + (LANES,))
+    near = near.T
 
     own_row = row_start + 4 * (ring % 4) + ring // 4
     around = lax.dynamic_slice_in_dim(rows, own_row + REACH, 1 + HALO, axis=1).T
@@ -280,11 +295,6 @@
         jnp.pad(shifts, (REACH, REACH)), own_row, 1 + HALO, axis=0
     )
     turn = jnp.concatenate([(turn + REACH) % (azi * LANES), turn[REACH : REACH + 1]])
-
-    whole, edge = call(
-        put_together, (f32(PLANES, TALL, LANES), f32(TALL, LANES)), [VMEM] * 3
-    )(state, below, above)
-    edge = lax.ppermute(edge, "azi", [((i + 1) % azi, i) for i in range(azi)])
 
     count = (4 + HALO) * PLANES
     tile = pltpu.VMEM((PLANES, TALL, 2 * LANES), jnp.float32)
@@ -292,16 +302,20 @@
         first_step,
         f32(4, count, LANES),
         [VMEM] * 3,
-        (tile, tile, tile, pltpu.VMEM((PACK * PLANES, LANES), jnp.float32)),
+        (
+            tile,
+            tile,
+            tile,
+            pltpu.VMEM((PACK * PLANES, LANES), jnp.float32),
+            pltpu.VMEM((near.shape[1], TALL, LANES), jnp.float32),
+        ),
     )(whole, edge, near)
     along_z = [[4 * x + z for z in range(4)] for x in range(4)]
     along_x = [[4 * x + z for x in range(4)] for z in range(4)]
     got = lax.all_to_all(sent, "azi", 0, 0, axis_index_groups=along_z)
     size = (1 + HALO) * PLANES
-    sent = call(spread, f32(4, 4, size, LANES), [VMEM])(got)
-    got = lax.all_to_all(
-        sent.reshape(4, 4 * size, LANES), "azi", 0, 0, axis_index_groups=along_x
-    )
+    sent = call(spread, f32(4, 4 * size, LANES), [VMEM])(got)
+    got = lax.all_to_all(sent, "azi", 0, 0, axis_index_groups=along_x)
     band = pltpu.VMEM((1 + HALO, PLANES, 16, LANES), jnp.float32)
     sent = call(
         second_step, f32(16 * PACK, LANES), [SMEM, SMEM, VMEM], (band, band, band)

time: 124 us -> 115 us (0.927)
  the two profiles are of different devices: /device:TPU:120 before, /device:TPU:24 now
where the time goes in v2:
time: 115 us; the launch traced here: 114 us
  blocking collectives  57.3 us (50%)
  starting transfers between devices  33.7 us (29%)
  waiting for transfers between devices  12 us (10%)
  Pallas kernels  6.08 us (5%)
  local copies, waits for them, and re-layouts  3.56 us (3%)
  other arithmetic  1.59 us (1%)
    all_to_all x1, blocking collectives, on_device(): got = lax.all_to_all(sent, 'azi', 0, 0, axis_index_groups=along_z)  31 us
    all_to_all x1, blocking collectives, on_device(): got = lax.all_to_all(sent.reshape(16, PACK, LANES), 'azi', 0, 0)  26.3 us
    ppermute x1, starting transfers between devices, on_device(): edge = lax.ppermute(edge, 'azi', [((i + 1) % azi, i) for i in range(azi)])  19.5 us
    all_to_all x1, waiting for transfers between devices, on_device(): got = lax.all_to_all(sent, 'azi', 0, 0, axis_index_groups=along_x)  10 us
    ppermute x1, starting transfers between devices, on_device(): lax.ppermute(state[:, :, 0:HALO, :], 'rad', [(i + 1, i) for i in range(ra...  7.22 us
    all_to_all x1, starting transfers between devices, on_device(): got = lax.all_to_all(sent, 'azi', 0, 0, axis_index_groups=along_x)  5.1 us
  transfers between devices with their start and end apart: 4, of which 3 were waited for; matrix products, arithmetic and copies ran while one was open for 3% of the time, Pallas kernels for 0%

profile of v2, /device:TPU:24, one launch (start us, length us, event | category | flops | bytes accessed | tf_op | source)
XLA Modules:
  0.0 114.3 jit_solution(15091638569207738520)
XLA Ops:
  0.0 0.9 fusion.2
  0.9 1.9 %collective-permute-start.1 = (f32[5,4,6,128]{3,2,1,0:T(8,128)S(1)}, f32[5,4,6,128]{3,2,1,0:T(8,128)S(1)}, u32[]{:S(2)}, u32[]{:S(2)}) collective-permute-start(f32[5,4,6,128]{3,2,1,0:T(8,128)S(1)} %get-tuple-element.21), channel_id=1, source_target_pairs={{0,16},{16,32},{32,48},{48,64},{64,80},{80,96},{96,112},{112,128},... | collective-permute-start | bytes 184328 | tf_op jit(solution)/shard_map/ppermute | solution.py:253
  2.9 7.2 %collective-permute-start = (f32[5,4,6,128]{3,2,1,0:T(8,128)S(1)}, f32[5,4,6,128]{3,2,1,0:T(8,128)S(1)}, u32[]{:S(2)}, u32[]{:S(2)}) collective-permute-start(f32[5,4,6,128]{3,2,1,0:T(8,128)S(1)} %get-tuple-element.22), channel_id=1, source_target_pairs={{16,0},{32,16},{48,32},{64,48},{80,64},{96,80},{112,96},{128,112},... | collective-permute-start | bytes 184328 | tf_op jit(solution)/shard_map/ppermute | solution.py:250
  10.1 0.1 pad.11.clone
  10.2 0.1 collective-permute-done.1.above
  10.3 1.9 %collective-permute-done.below = f32[5,4,6,128]{3,2,1,0:T(8,128)S(1)} collective-permute-done((f32[5,4,6,128]{3,2,1,0:T(8,128)S(1)}, f32[5,4,6,128]{3,2,1,0:T(8,128)S(1)}, u32[]{:S(2)}, u32[]{:S(2)}) %collective-permute-start) | collective-permute-done | bytes 61472 | tf_op jit(solution)/shard_map/ppermute | solution.py:250
  12.1 0.0 copy-start
  12.1 0.9 copy-done
  13.1 0.2 put_together.1
  13.2 19.5 %collective-permute-start.2 = (f32[32,128]{1,0:T(8,128)S(1)}, f32[32,128]{1,0:T(8,128)S(1)}, u32[]{:S(2)}, u32[]{:S(2)}) collective-permute-start(f32[32,128]{1,0:T(8,128)S(1)} %get-tuple-element.18), channel_id=1, source_target_pairs={{1,0},{2,1},{3,2},{4,3},{5,4},{6,5},{7,6},{8,7},{9,8},{10,9},{11,1... | collective-permute-start | bytes 49160 | tf_op jit(solution)/shard_map/ppermute | solution.py:263
  32.7 0.7 multiply_add_fusion
  33.4 0.8 concatenate.10
  34.2 0.2 copy.12
  34.5 0.1 maximum_bitcast_fusion.row_ref
  34.6 0.0 collective-permute-done.2.edge_ref
  34.6 1.9 %first_step.1 = f32[4,200,128]{2,1,0:T(8,128)S(1)} custom-call(f32[20,32,128]{2,1,0:T(8,128)S(1)} %get-tuple-element.17.all_ref, f32[32,128]{1,0:T(8,128)S(1)} %collective-permute-done.2.edge_ref, f32[32,9]{1,0:T(8,128)S(1)} %maximum_bitcast_fusion.row_ref), custom_call_target="tpu_custom_call" | custom-call | tf_op jit(solution)/shard_map/first_step/pallas_call | solution.py:301
  36.5 31.0 %all_to_all.15.got_ref = f32[4,200,128]{2,1,0:T(8,128)S(1)} all-to-all(f32[4,200,128]{2,1,0:T(8,128)S(1)} %first_step.1), channel_id=1, replica_groups={{0,1,2,3},{4,5,6,7},{8,9,10,11},{12,13,14,15},{16,17,18,19},{20,21,22,2..., dimensions={0} | all-to-all | bytes 819200 | tf_op jit(solution)/shard_map/all_to_all | solution.py:315
  67.6 1.1 spread.1
  68.7 0.0 copy-start.1
  68.7 5.1 %all-to-all-start.1 = ((f32[4,560,128]{2,1,0:T(8,128)}), f32[4,560,128]{2,1,0:T(8,128)S(1)}, u32[]{:S(2)}, u32[]{:S(2)}) async-start(f32[4,560,128]{2,1,0:T(8,128)} %spread.1), calls=%async_computation.1 | async-start | bytes 2293760 | tf_op jit(solution)/shard_map/all_to_all | solution.py:318
  73.8 0.0 copy-done.1
  73.8 0.1 and_select_fusion
  73.8 0.6 slice.17
  74.4 0.7 pad_add_fusion.amount_ref
  75.2 10.0 %all-to-all-done.1 = f32[4,560,128]{2,1,0:T(8,128)S(1)} async-done(((f32[4,560,128]{2,1,0:T(8,128)}), f32[4,560,128]{2,1,0:T(8,128)S(1)}, u32[]{:S(2)}, u32[]{:S(2)}) %all-to-all-start.1) | async-done | bytes 1146912 | tf_op jit(solution)/shard_map/all_to_all | solution.py:318
  85.2 2.1 %second_step.1 = f32[384,128]{1,0:T(8,128)S(1)} custom-call(s32[8]{0:T(128)S(1)} %pad_add_fusion.amount_ref, f32[7,9]{1,0:T(8,128)S(1)} %fusion.coef_ref, f32[2240,128]{1,0:T(8,128)S(1)} %bitcast.11), custom_call_target="tpu_custom_call" | custom-call | tf_op jit(solution)/shard_map/second_step/pallas_call | solution.py:320
  87.3 26.3 %all_to_all.16 = f32[16,24,128]{2,1,0:T(8,128)S(1)} all-to-all(f32[16,24,128]{2,1,0:T(8,128)S(1)} %bitcast.12), channel_id=1, replica_groups=mesh['rad'=64,'azi'=16] {'azi'}, dimensions={0} | all-to-all | bytes 393216 | tf_op jit(solution)/shard_map/all_to_all | solution.py:323
  113.6 0.8 set_down.1
  (5 shorter events, 0.1 us)
Async XLA Ops:
  0.9 9.3 %collective-permute-start.1 = (f32[5,4,6,128]{3,2,1,0:T(8,128)S(1)}, f32[5,4,6,128]{3,2,1,0:T(8,128)S(1)}, u32[]{:S(2)}, u32[]{:S(2)}) collective-permute-start(f32[5,4,6,128]{3,2,1,0:T(8,128)S(1)} %get-tuple-element.21), channel_id=1, source_target_pairs={{0,16},{16,32},{32,48},{48,64},{64,80},{80,96},{96,112},{112,128},... | collective-permute-start | bytes 184328 | tf_op jit(solution)/shard_map/ppermute | solution.py:253
  2.9 9.3 %collective-permute-start = (f32[5,4,6,128]{3,2,1,0:T(8,128)S(1)}, f32[5,4,6,128]{3,2,1,0:T(8,128)S(1)}, u32[]{:S(2)}, u32[]{:S(2)}) collective-permute-start(f32[5,4,6,128]{3,2,1,0:T(8,128)S(1)} %get-tuple-element.22), channel_id=1, source_target_pairs={{16,0},{32,16},{48,32},{64,48},{80,64},{96,80},{112,96},{128,112},... | collective-permute-start | bytes 184328 | tf_op jit(solution)/shard_map/ppermute | solution.py:250
  12.1 0.9 copy-start
  13.2 21.4 %collective-permute-start.2 = (f32[32,128]{1,0:T(8,128)S(1)}, f32[32,128]{1,0:T(8,128)S(1)}, u32[]{:S(2)}, u32[]{:S(2)}) collective-permute-start(f32[32,128]{1,0:T(8,128)S(1)} %get-tuple-element.18), channel_id=1, source_target_pairs={{1,0},{2,1},{3,2},{4,3},{5,4},{6,5},{7,6},{8,7},{9,8},{10,9},{11,1... | collective-permute-start | bytes 49160 | tf_op jit(solution)/shard_map/ppermute | solution.py:263
  68.7 5.1 %copy-start.1 = (s32[1024]{0:T(1024)S(1)}, s32[1024]{0:T(1024)}, u32[]{:S(2)}) copy-start(s32[1024]{0:T(1024)} %param.6) | copy-start | bytes 12292
  68.7 16.5 %all-to-all-start.1 = ((f32[4,560,128]{2,1,0:T(8,128)}), f32[4,560,128]{2,1,0:T(8,128)S(1)}, u32[]{:S(2)}, u32[]{:S(2)}) async-start(f32[4,560,128]{2,1,0:T(8,128)} %spread.1), calls=%async_computation.1 | async-start | bytes 2293760 | tf_op jit(solution)/shard_map/all_to_all | solution.py:318

commit v3 on v1

--- a/solution.py
+++ b/solution.py
@@ -20,26 +20,17 @@
 HALO = 2 * REACH
 TALL = 32
 PACK = 24
-
-
-def put_together(main, below, above, all_ref, edge_ref):
-    lane = lax.broadcasted_iota(jnp.int32, (TALL, LANES), 1)
-    edge = jnp.zeros((TALL, LANES), jnp.float32)
+HELD = PLANES + 1
+BAND = (1 + HALO) * HELD + 1
+ROOM = 16 * 1024 * 1024
+
+
+def cut(main_ref, low_ref, high_ref, kept_ref):
     for plane in range(PLANES):
         f, k = divmod(plane, LEVELS)
-        all_ref[plane, 0:ROWS, :] = main[f, k]
-        all_ref[plane, ROWS : ROWS + HALO, :] = below[f, k]
-        all_ref[plane, ROWS + HALO : TALL - HALO, :] = jnp.zeros(
-            (TALL - ROWS - 2 * HALO, LANES), jnp.float32
-        )
-        all_ref[plane, TALL - HALO : TALL, :] = above[f, k]
-    for plane in range(PLANES):
-        cells = all_ref[plane]
-        if plane:
-            cells = pltpu.roll(cells, HALO * plane, 1)
-        here = (lane >= HALO * plane) & (lane < HALO * (plane + 1))
-        edge = jnp.where(here, cells, edge)
-    edge_ref[...] = edge
+        low_ref[f, k] = main_ref[f, k, 0:HALO]
+        high_ref[f, k] = main_ref[f, k, ROWS - HALO : ROWS]
+        kept_ref[f, k] = main_ref[f, k]
 
 
 def advance(at, slopes, coefs):
@@ -78,14 +69,69 @@
     return start * (1.0 / 3.0) + (2.0 / 3.0) * (now + change)
 
 
-def first_step(all_ref, edge_ref, coef_ref, send_ref, begin, one, two, table):
+def row_values(
+    spin_hbm, drift_hbm, stiff_hbm, coef_ref, spin_ref, drift_ref, stiff_ref, sems
+):
+    copies = [
+        pltpu.make_async_copy(source, target, sems.at[i])
+        for i, (source, target) in enumerate(
+            ((spin_hbm, spin_ref), (drift_hbm, drift_ref), (stiff_hbm, stiff_ref))
+        )
+    ]
+    for copy in copies:
+        copy.start()
+    for copy in copies:
+        copy.wait()
     wide = 2 * LANES
-    edge = edge_ref[...]
+    total = spin_ref.shape[1]
+    row_start = lax.axis_index("rad") * ROWS
+    seen = lax.rem(row_start - HALO + total, total)
+    here = pl.multiple_of(seen // LANES * LANES, LANES)
+    after = pl.multiple_of(lax.rem(here + LANES, total), LANES)
+    back = lax.rem(wide - lax.rem(seen, LANES), wide)
+
+    def column(ref, i):
+        pair = [ref[i : i + 1, pl.ds(start, LANES)] for start in (here, after)]
+        pair = jnp.concatenate(pair, axis=1)
+        pair = jnp.broadcast_to(pair, (8, wide))
+        tall = jnp.transpose(pltpu.roll(pair, back, 1)[:, 0:LANES])[0:TALL]
+        tall = pltpu.roll(tall, TALL - HALO, 0)
+        return jnp.broadcast_to(tall[:, 0:1], (TALL, LANES))
+
+    spin, drift = column(spin_ref, 0), column(drift_ref, 0)
+    coef_ref[0] = NEAR - HD * drift
+    coef_ref[1] = NEAR + HD * drift
+    coef_ref[2] = (2.0 * DT) * spin
+    coef_ref[3] = (0.5 * DT) * spin
+    for k in range(LEVELS):
+        coef_ref[4 + k] = column(stiff_ref, k)
+    local = lax.broadcasted_iota(jnp.int32, (TALL, LANES), 0)
+    local = row_start + jnp.where(local < ROWS + HALO, local, local - TALL)
+    inside = (local >= 0) & (local < total)
+    coef_ref[4 + LEVELS] = jnp.where(inside, 1.0, 0.0)
+
+
+def first_step(
+    main_ref,
+    below_ref,
+    above_ref,
+    coef_ref,
+    send_ref,
+    begin,
+    one,
+    two,
+    table,
+):
+    wide = 2 * LANES
     for plane in range(PLANES):
-        begin[plane, :, 0:LANES] = all_ref[plane]
-        begin[plane, :, LANES:wide] = (
-            pltpu.roll(edge, LANES - HALO * plane, 1) if plane else edge
-        )
+        f, k = divmod(plane, LEVELS)
+        begin[plane, 0:ROWS, 0:LANES] = main_ref[f, k]
+        begin[plane, ROWS : ROWS + HALO, 0:LANES] = below_ref[f, k]
+        begin[plane, ROWS + HALO : TALL - HALO, 0:LANES] = jnp.zeros(
+            (TALL - ROWS - 2 * HALO, LANES), jnp.float32
+        )
+        begin[plane, TALL - HALO : TALL, 0:LANES] = above_ref[f, k]
+        begin[plane, :, LANES:wide] = jnp.zeros((TALL, LANES), jnp.float32)
 
     def coef(i):
         part = coef_ref[i]
@@ -94,6 +140,7 @@
     sources = (begin, one, two)
     targets = (one, two, None)
     lane = lax.broadcasted_iota(jnp.int32, (TALL, LANES), 1)
+    spill = jnp.zeros((TALL, LANES), jnp.float32)
     for stage in range(3):
         src, dst = sources[stage], targets[stage]
         for k in range(LEVELS):
@@ -124,21 +171,34 @@
                 if dst is not None:
                     dst[plane] = value
                 else:
-                    left = pltpu.roll(value[:, 0:LANES], LANES - REACH, 1)
-                    right = pltpu.roll(value[:, LANES:wide], LANES - REACH, 1)
-                    shown = jnp.where(lane < LANES - REACH, left, right)
-                    shown = pltpu.roll(shown, REACH, 0)
-                    table[pl.ds(plane, PACK, PLANES), :] = shown[0:PACK]
-    size = (4 + HALO) * PLANES
+                    table[pl.ds(plane, PACK, HELD), :] = pltpu.roll(
+                        value[:, 0:LANES], REACH, 0
+                    )[0:PACK]
+                    past = pltpu.roll(
+                        value[:, LANES:wide], (HALO * plane + REACH) % LANES, 1
+                    )
+                    mine = (lane >= HALO * plane) & (lane < HALO * (plane + 1))
+                    spill = jnp.where(mine, past, spill)
+    table[pl.ds(PLANES, PACK, HELD), :] = pltpu.roll(spill, REACH, 0)[0:PACK]
+    size = (4 + HALO) * HELD
     for group in range(4):
-        send_ref[group] = table[group * 4 * PLANES : group * 4 * PLANES + size]
+        send_ref[group, 0:size, :] = table[group * 4 * HELD : group * 4 * HELD + size]
+        send_ref[group, size:, :] = jnp.zeros(
+            (send_ref.shape[1] - size, LANES), jnp.float32
+        )
 
 
 def spread(got_ref, send_ref):
-    size = (1 + HALO) * PLANES
+    size = (1 + HALO) * HELD
     for target in range(4):
         for z in range(4):
-            send_ref[target, z] = got_ref[z, target * PLANES : target * PLANES + size]
+            start = z * BAND
+            send_ref[target, start : start + size, :] = got_ref[
+                z, target * HELD : target * HELD + size, :
+            ]
+            send_ref[target, start + size : start + BAND, :] = jnp.zeros(
+                (BAND - size, LANES), jnp.float32
+            )
 
 
 def turned(cells, amount, lane):
@@ -152,16 +212,25 @@
 
 def second_step(amount_ref, coef_ref, got_ref, send_ref, begin, one, two):
     lane = lax.broadcasted_iota(jnp.int32, (16, LANES), 1)
+    edge = (lane < REACH) | (lane >= LANES - REACH)
     span = 1 + HALO
     for row in range(span):
         amount = amount_ref[row]
+        spill = got_ref[pl.ds(row * HELD + PLANES, 16, BAND), :]
+        spill = jnp.where(
+            lax.rem(lane, HALO) < REACH,
+            pltpu.roll(spill, 15, 0),
+            pltpu.roll(spill, 1, 0),
+        )
         for plane in range(PLANES):
-            cells = got_ref[pl.ds(row * PLANES + plane, 16, span * PLANES), :]
+            cells = got_ref[pl.ds(row * HELD + plane, 16, BAND), :]
+            past = pltpu.roll(spill, LANES - REACH - HALO * plane, 1)
+            cells = cells + jnp.where(edge, past, 0.0)
             begin[row, plane] = turned(cells, amount, lane)
 
     sources = (begin, one, two)
     targets = (one, two, None)
-    last_amount = amount_ref[span]
+    last_amount = amount_ref[REACH]
     for stage in range(3):
         src, dst = sources[stage], targets[stage]
         for row in range(stage + 1, span - 1 - stage):
@@ -230,23 +299,53 @@
         in_specs=in_specs,
         out_specs=(VMEM,) * len(out_shape) if many else VMEM,
         scratch_shapes=list(scratch),
+        compiler_params=pltpu.CompilerParams(vmem_limit_bytes=ROOM),
     )
 
 
 def on_device(state, shifts, spin, drift, stiffness):
     rad = lax.axis_size("rad")
-    azi = lax.axis_size("azi")
     ring = lax.axis_index("azi")
     total = spin.shape[0]
     row_start = lax.axis_index("rad") * ROWS
 
-    below = lax.ppermute(
-        state[:, :, 0:HALO, :], "rad", [(i + 1, i) for i in range(rad - 1)]
-    )
-    above = lax.ppermute(
-        state[:, :, ROWS - HALO :, :], "rad", [(i, i + 1) for i in range(rad - 1)]
-    )
-
+    few = f32(FIELDS, LEVELS, HALO, LANES)
+    low, high, state = call(cut, (few, few, f32(*state.shape)), [VMEM])(state)
+    spin, drift, stiffness, low, high = lax.optimization_barrier(
+        (spin, drift, stiffness, low, high)
+    )
+    coefs = call(
+        row_values,
+        f32(5 + LEVELS, TALL, LANES),
+        [pl.BlockSpec(memory_space=pltpu.HBM)] * 3,
+        (
+            pltpu.VMEM((1, total), jnp.float32),
+            pltpu.VMEM((1, total), jnp.float32),
+            pltpu.VMEM((LEVELS, total), jnp.float32),
+            pltpu.SemaphoreType.DMA((3,)),
+        ),
+    )(spin[None], drift[None], stiffness)
+    below = lax.ppermute(low, "rad", [(i + 1, i) for i in range(rad - 1)])
+    above = lax.ppermute(high, "rad", [(i, i + 1) for i in range(rad - 1)])
+
+    count = (4 + HALO) * HELD
+    count += -count % 8
+    tile = pltpu.VMEM((PLANES, TALL, 2 * LANES), jnp.float32)
+    sent = call(
+        first_step,
+        f32(4, count, LANES),
+        [VMEM] * 4,
+        (tile, tile, tile, pltpu.VMEM((PACK * HELD, LANES), jnp.float32)),
+    )(state, below, above, coefs)
+    along_z = [[4 * x + z for z in range(4)] for x in range(4)]
+    along_x = [[4 * x + z for x in range(4)] for z in range(4)]
+    got = lax.all_to_all(sent, "azi", 0, 0, axis_index_groups=along_z)
+    sent = call(spread, f32(4, 4 * BAND, LANES), [VMEM])(got)
+
+    spin, drift, stiffness, shifts, sent = lax.optimization_barrier(
+        (spin, drift, stiffness, shifts, sent)
+    )
+    own_row = row_start + 4 * (ring % 4) + ring // 4
     rows = jnp.concatenate(
         [
             jnp.stack(
@@ -262,50 +361,17 @@
         ],
         axis=0,
     )
-    rows = jnp.pad(rows, ((0, 0), (HALO, HALO)))
-    near = lax.dynamic_slice_in_dim(rows, row_start, ROWS + 2 * HALO, axis=1)
-    near = jnp.concatenate(
-        [
-            near[:, HALO:],
-            jnp.zeros((rows.shape[0], TALL - ROWS - 2 * HALO), jnp.float32),
-            near[:, :HALO],
-        ],
-        axis=1,
-    )
-    near = jnp.broadcast_to(near[:, :, None], near.shape + (LANES,))
-
-    own_row = row_start + 4 * (ring % 4) + ring // 4
-    around = lax.dynamic_slice_in_dim(rows, own_row + REACH, 1 + HALO, axis=1).T
+    rows = jnp.pad(rows, ((0, 0), (REACH, REACH)))
+    around = lax.dynamic_slice_in_dim(rows, own_row, 1 + HALO, axis=1).T
     turn = lax.dynamic_slice_in_dim(
         jnp.pad(shifts, (REACH, REACH)), own_row, 1 + HALO, axis=0
     )
-    turn = jnp.concatenate([(turn + REACH) % (azi * LANES), turn[REACH : REACH + 1]])
-
-    whole, edge = call(
-        put_together, (f32(PLANES, TALL, LANES), f32(TALL, LANES)), [VMEM] * 3
-    )(state, below, above)
-    edge = lax.ppermute(edge, "azi", [((i + 1) % azi, i) for i in range(azi)])
-
-    count = (4 + HALO) * PLANES
-    tile = pltpu.VMEM((PLANES, TALL, 2 * LANES), jnp.float32)
-    sent = call(
-        first_step,
-        f32(4, count, LANES),
-        [VMEM] * 3,
-        (tile, tile, tile, pltpu.VMEM((PACK * PLANES, LANES), jnp.float32)),
-    )(whole, edge, near)
-    along_z = [[4 * x + z for z in range(4)] for x in range(4)]
-    along_x = [[4 * x + z for x in range(4)] for z in range(4)]
-    got = lax.all_to_all(sent, "azi", 0, 0, axis_index_groups=along_z)
-    size = (1 + HALO) * PLANES
-    sent = call(spread, f32(4, 4, size, LANES), [VMEM])(got)
-    got = lax.all_to_all(
-        sent.reshape(4, 4 * size, LANES), "azi", 0, 0, axis_index_groups=along_x
-    )
+
+    got = lax.all_to_all(sent, "azi", 0, 0, axis_index_groups=along_x)
     band = pltpu.VMEM((1 + HALO, PLANES, 16, LANES), jnp.float32)
     sent = call(
         second_step, f32(16 * PACK, LANES), [SMEM, SMEM, VMEM], (band, band, band)
-    )(turn, around, got.reshape(16 * size, LANES))
+    )(turn, around, got.reshape(16 * BAND, LANES))
     got = lax.all_to_all(sent.reshape(16, PACK, LANES), "azi", 0, 0)
     return call(set_down, f32(FIELDS, LEVELS, ROWS, LANES), [VMEM])(
         got.reshape(16 * PACK, LANES)

time: 124 us -> 113 us (0.911)
  the two profiles are of different devices: /device:TPU:120 before, /device:TPU:56 now
where the time goes in v3:
time: 113 us; the launch traced here: 111 us
  blocking collectives  58.3 us (52%)
  waiting for transfers between devices  20 us (18%)
  Pallas kernels  14.5 us (13%)
  starting transfers between devices  14.5 us (13%)
  local copies, waits for them, and re-layouts  3.39 us (3%)
    all_to_all x1, blocking collectives, on_device(): got = lax.all_to_all(sent, 'azi', 0, 0, axis_index_groups=along_z)  34.5 us
    all_to_all x1, blocking collectives, on_device(): got = lax.all_to_all(sent.reshape(16, PACK, LANES), 'azi', 0, 0)  23.8 us
    all_to_all x1, waiting for transfers between devices, on_device(): got = lax.all_to_all(sent, 'azi', 0, 0, axis_index_groups=along_x)  15.9 us
    pallas_call x1, Pallas kernels, on_device(): call(second_step, f32(16 * PACK, LANES), [SMEM, SMEM, VMEM], (band, band,...  10.4 us
    ppermute x1, starting transfers between devices, on_device(): below = lax.ppermute(low, 'rad', [(i + 1, i) for i in range(rad - 1)])  8.12 us
    all_to_all x1, starting transfers between devices, on_device(): got = lax.all_to_all(sent, 'azi', 0, 0, axis_index_groups=along_x)  4.44 us
    ppermute x1, waiting for transfers between devices, on_device(): above = lax.ppermute(high, 'rad', [(i, i + 1) for i in range(rad - 1)])  4.1 us
    unnamed x16, local copies, waits for them, and re-layouts  3.02 us
  transfers between devices with their start and end apart: 3, of which 2 were waited for; matrix products, arithmetic and copies ran while one was open for 0% of the time, Pallas kernels for 0%

profile of v3, /device:TPU:56, one launch (start us, length us, event | category | flops | bytes accessed | tf_op | source)
XLA Modules:
  0.0 110.7 jit_solution(1678031300287933788)
XLA Ops:
  0.0 0.0 copy-start
  0.0 0.9 copy-done
  0.9 8.1 %collective-permute-start = (f32[5,4,6,128]{3,2,1,0:T(8,128)S(1)}, f32[5,4,6,128]{3,2,1,0:T(8,128)S(1)}, u32[]{:S(2)}, u32[]{:S(2)}) collective-permute-start(f32[5,4,6,128]{3,2,1,0:T(8,128)S(1)} %get-tuple-element.24), channel_id=1, source_target_pairs={{16,0},{32,16},{48,32},{64,48},{80,64},{96,80},{112,96},{128,112},... | collective-permute-start | bytes 184328 | tf_op jit(solution)/shard_map/ppermute | solution.py:328
  9.1 1.9 %collective-permute-start.1 = (f32[5,4,6,128]{3,2,1,0:T(8,128)S(1)}, f32[5,4,6,128]{3,2,1,0:T(8,128)S(1)}, u32[]{:S(2)}, u32[]{:S(2)}) collective-permute-start(f32[5,4,6,128]{3,2,1,0:T(8,128)S(1)} %get-tuple-element.25), channel_id=1, source_target_pairs={{0,16},{16,32},{32,48},{48,64},{64,80},{80,96},{96,112},{112,128},... | collective-permute-start | bytes 184328 | tf_op jit(solution)/shard_map/ppermute | solution.py:329
  11.0 0.0 copy-start.1
  11.0 0.7 copy-done.1
  11.7 0.0 copy-start.3
  11.7 0.7 copy-done.3
  12.4 0.0 copy-start.5
  12.4 0.7 copy-done.5
  13.1 0.3 row_values.1.coef_ref
  13.4 0.0 collective-permute-done.below_ref
  13.4 4.1 %collective-permute-done.1.above_ref = f32[5,4,6,128]{3,2,1,0:T(8,128)S(1)} collective-permute-done((f32[5,4,6,128]{3,2,1,0:T(8,128)S(1)}, f32[5,4,6,128]{3,2,1,0:T(8,128)S(1)}, u32[]{:S(2)}, u32[]{:S(2)}) %collective-permute-start.1) | collective-permute-done | bytes 61472 | tf_op jit(solution)/shard_map/ppermute | solution.py:329
  17.5 1.8 %first_step.1 = f32[4,216,128]{2,1,0:T(8,128)S(1)} custom-call(f32[5,4,16,128]{3,2,1,0:T(8,128)S(1)} %get-tuple-element.23.main_ref, f32[5,4,6,128]{3,2,1,0:T(8,128)S(1)} %collective-permute-done.below_ref, f32[5,4,6,128]{3,2,1,0:T(8,128)S(1)} %collective-permute-done.1.above_ref, f32[9,32,128]{2,1,0:T(8,128)S(1)} %row_values.1.coef_ref), custom_call_target="tpu_custom_call" | custom-call | tf_op jit(solution)/shard_map/first_step/pallas_call | solution.py:334
  19.3 34.5 %all_to_all.15.got_ref = f32[4,216,128]{2,1,0:T(8,128)S(1)} all-to-all(f32[4,216,128]{2,1,0:T(8,128)S(1)} %first_step.1), channel_id=1, replica_groups={{0,1,2,3},{4,5,6,7},{8,9,10,11},{12,13,14,15},{16,17,18,19},{20,21,22,2..., dimensions={0} | all-to-all | bytes 884736 | tf_op jit(solution)/shard_map/all_to_all | solution.py:342
  53.8 1.1 %spread.1 = f32[4,592,128]{2,1,0:T(8,128)} custom-call(f32[4,216,128]{2,1,0:T(8,128)S(1)} %all_to_all.15.got_ref), custom_call_target="tpu_custom_call" | custom-call | tf_op jit(solution)/shard_map/spread/pallas_call | solution.py:343
  54.9 0.0 copy-start.4
  54.9 0.0 copy-start.6
  54.9 0.0 copy-start.2
  54.9 0.0 copy-start.7
  54.9 4.4 %all-to-all-start.1 = ((f32[4,592,128]{2,1,0:T(8,128)}), f32[4,592,128]{2,1,0:T(8,128)S(1)}, u32[]{:S(2)}, u32[]{:S(2)}) async-start(f32[4,592,128]{2,1,0:T(8,128)} %spread.1), calls=%async_computation.1 | async-start | bytes 2424832 | tf_op jit(solution)/shard_map/all_to_all | solution.py:370
  59.4 0.0 copy-done.4
  59.4 0.0 copy-done.6
  59.4 0.0 copy-done.2
  59.4 0.1 concatenate.3
  59.5 0.2 copy.12
  59.7 0.0 copy-done.7
  59.7 0.1 pad_dynamic-slice_fusion.1.amount_ref
  59.8 15.9 %all-to-all-done.1 = f32[4,592,128]{2,1,0:T(8,128)S(1)} async-done(((f32[4,592,128]{2,1,0:T(8,128)}), f32[4,592,128]{2,1,0:T(8,128)S(1)}, u32[]{:S(2)}, u32[]{:S(2)}) %all-to-all-start.1) | async-done | bytes 1212448 | tf_op jit(solution)/shard_map/all_to_all | solution.py:370
  75.7 10.4 %second_step.1 = f32[384,128]{1,0:T(8,128)S(1)} custom-call(s32[7]{0:T(128)S(1)} %pad_dynamic-slice_fusion.1.amount_ref, f32[7,9]{1,0:T(8,128)S(1)} %fusion.coef_ref, f32[2368,128]{1,0:T(8,128)S(1)} %bitcast.11), custom_call_target="tpu_custom_call" | custom-call | tf_op jit(solution)/shard_map/second_step/pallas_call | solution.py:372
  86.2 23.8 %all_to_all.16 = f32[16,24,128]{2,1,0:T(8,128)S(1)} all-to-all(f32[16,24,128]{2,1,0:T(8,128)S(1)} %bitcast.12), channel_id=1, replica_groups=mesh['rad'=64,'azi'=16] {'azi'}, dimensions={0} | all-to-all | bytes 393216 | tf_op jit(solution)/shard_map/all_to_all | solution.py:375
  110.0 0.8 set_down.1
  (4 shorter events, 0.0 us)
Async XLA Ops:
  0.0 0.9 copy-start
  0.9 12.5 %collective-permute-start = (f32[5,4,6,128]{3,2,1,0:T(8,128)S(1)}, f32[5,4,6,128]{3,2,1,0:T(8,128)S(1)}, u32[]{:S(2)}, u32[]{:S(2)}) collective-permute-start(f32[5,4,6,128]{3,2,1,0:T(8,128)S(1)} %get-tuple-element.24), channel_id=1, source_target_pairs={{16,0},{32,16},{48,32},{64,48},{80,64},{96,80},{112,96},{128,112},... | collective-permute-start | bytes 184328 | tf_op jit(solution)/shard_map/ppermute | solution.py:328
  9.1 8.5 %collective-permute-start.1 = (f32[5,4,6,128]{3,2,1,0:T(8,128)S(1)}, f32[5,4,6,128]{3,2,1,0:T(8,128)S(1)}, u32[]{:S(2)}, u32[]{:S(2)}) collective-permute-start(f32[5,4,6,128]{3,2,1,0:T(8,128)S(1)} %get-tuple-element.25), channel_id=1, source_target_pairs={{0,16},{16,32},{32,48},{48,64},{64,80},{80,96},{96,112},{112,128},... | collective-permute-start | bytes 184328 | tf_op jit(solution)/shard_map/ppermute | solution.py:329
  11.0 0.7 copy-start.1
  11.7 0.7 copy-start.3
  12.4 0.7 copy-start.5
  54.9 4.5 %copy-start.4 = (f32[1024]{0:T(1024)S(1)}, f32[1024]{0:T(1024)}, u32[]{:S(2)}) copy-start(f32[1024]{0:T(1024)} %param.8) | copy-start | bytes 12292
  54.9 4.5 %copy-start.6 = (f32[1024]{0:T(1024)S(1)}, f32[1024]{0:T(1024)}, u32[]{:S(2)}) copy-start(f32[1024]{0:T(1024)} %param.7) | copy-start | bytes 12292
  54.9 4.5 %copy-start.2 = (f32[4,1024]{1,0:T(4,128)S(1)}, f32[4,1024]{1,0:T(4,128)}, u32[]{:S(2)}) copy-start(f32[4,1024]{1,0:T(4,128)} %stiff_hbm) | copy-start | bytes 49156
  54.9 4.8 %copy-start.7 = (s32[1024]{0:T(1024)S(1)}, s32[1024]{0:T(1024)}, u32[]{:S(2)}) copy-start(s32[1024]{0:T(1024)} %param.6) | copy-start | bytes 12292
  54.9 20.8 %all-to-all-start.1 = ((f32[4,592,128]{2,1,0:T(8,128)}), f32[4,592,128]{2,1,0:T(8,128)S(1)}, u32[]{:S(2)}, u32[]{:S(2)}) async-start(f32[4,592,128]{2,1,0:T(8,128)} %spread.1), calls=%async_computation.1 | async-start | bytes 2424832 | tf_op jit(solution)/shard_map/all_to_all | solution.py:370

commit v4 on v3

--- a/solution.py
+++ b/solution.py
@@ -213,28 +213,34 @@
 def second_step(amount_ref, coef_ref, got_ref, send_ref, begin, one, two):
     lane = lax.broadcasted_iota(jnp.int32, (16, LANES), 1)
     edge = (lane < REACH) | (lane >= LANES - REACH)
+    leftward = lax.rem(lane, HALO) < REACH
     span = 1 + HALO
-    for row in range(span):
+
+    def take(row, carry):
         amount = amount_ref[row]
-        spill = got_ref[pl.ds(row * HELD + PLANES, 16, BAND), :]
+        first = row * HELD
+        spill = got_ref[pl.ds(first + PLANES, 16, BAND), :]
         spill = jnp.where(
-            lax.rem(lane, HALO) < REACH,
-            pltpu.roll(spill, 15, 0),
-            pltpu.roll(spill, 1, 0),
+            leftward, pltpu.roll(spill, 15, 0), pltpu.roll(spill, 1, 0)
         )
         for plane in range(PLANES):
-            cells = got_ref[pl.ds(row * HELD + plane, 16, BAND), :]
+            cells = got_ref[pl.ds(first + plane, 16, BAND), :]
             past = pltpu.roll(spill, LANES - REACH - HALO * plane, 1)
             cells = cells + jnp.where(edge, past, 0.0)
             begin[row, plane] = turned(cells, amount, lane)
+        return carry
+
+    lax.fori_loop(0, span, take, 0)
 
     sources = (begin, one, two)
     targets = (one, two, None)
     last_amount = amount_ref[REACH]
     for stage in range(3):
         src, dst = sources[stage], targets[stage]
-        for row in range(stage + 1, span - 1 - stage):
+
+        def section(row, carry, stage=stage, src=src, dst=dst):
             scalars = [coef_ref[row, i] for i in range(5 + LEVELS)]
+            inside = scalars[4 + LEVELS] > 0.5
             for k in range(LEVELS):
 
                 def slopes(f):
@@ -259,18 +265,18 @@
                 for f in range(FIELDS):
                     plane = f * LEVELS + k
                     value = combine(stage, begin[row, plane], src[row, plane], change[f])
-                    if row != REACH:
-                        value = jnp.where(scalars[4 + LEVELS] > 0.5, value, 0.0)
                     if dst is not None:
-                        dst[row, plane] = value
+                        dst[row, plane] = jnp.where(inside, value, 0.0)
                     else:
-                        send_ref[pl.ds(plane, 16, PACK), :] = turned(
+                        send_ref[pl.ds(plane, 16, PLANES), :] = turned(
                             value, last_amount, lane
                         )
-    for j in range(16):
-        send_ref[j * PACK + PLANES : (j + 1) * PACK, :] = jnp.zeros(
-            (PACK - PLANES, LANES), jnp.float32
-        )
+            return carry
+
+        if dst is not None:
+            lax.fori_loop(stage + 1, span - 1 - stage, section, 0)
+        else:
+            section(REACH, 0)
 
 
 def set_down(got_ref, out_ref):
@@ -278,7 +284,7 @@
         f, k = divmod(plane, LEVELS)
         for z in range(4):
             out_ref[f, k, 4 * z : 4 * z + 4, :] = got_ref[
-                pl.ds(z * PACK + plane, 4, 4 * PACK), :
+                pl.ds(z * PLANES + plane, 4, 4 * PLANES), :
             ]
 
 
@@ -370,11 +376,11 @@
     got = lax.all_to_all(sent, "azi", 0, 0, axis_index_groups=along_x)
     band = pltpu.VMEM((1 + HALO, PLANES, 16, LANES), jnp.float32)
     sent = call(
-        second_step, f32(16 * PACK, LANES), [SMEM, SMEM, VMEM], (band, band, band)
+        second_step, f32(16 * PLANES, LANES), [SMEM, SMEM, VMEM], (band, band, band)
     )(turn, around, got.reshape(16 * BAND, LANES))
-    got = lax.all_to_all(sent.reshape(16, PACK, LANES), "azi", 0, 0)
+    got = lax.all_to_all(sent.reshape(16, FIELDS, LEVELS, LANES), "azi", 0, 0)
     return call(set_down, f32(FIELDS, LEVELS, ROWS, LANES), [VMEM])(
-        got.reshape(16 * PACK, LANES)
+        got.reshape(16 * PLANES, LANES)
     )
 
 

time: 113 us -> 105 us (0.929)
  Pallas kernels: 14.5 us -> 7.5 us
    pallas_call x1, Pallas kernels: 10.4 us -> 3.52 us  [on_device(): call(second_step, f32(16 * PLANES, LANES), [SMEM, SMEM, VMEM], (band, ban...]
where the time goes in v4:
time: 105 us; the launch traced here: 104 us
  blocking collectives  58.1 us (55%)
  waiting for transfers between devices  20 us (19%)
  starting transfers between devices  14.5 us (14%)
  Pallas kernels  7.5 us (7%)
  local copies, waits for them, and re-layouts  3.39 us (3%)
    all_to_all x1, blocking collectives, on_device(): got = lax.all_to_all(sent, 'azi', 0, 0, axis_index_groups=along_z)  34.5 us
    all_to_all x1, blocking collectives, on_device(): got = lax.all_to_all(sent.reshape(16, FIELDS, LEVELS, LANES), 'azi', 0, 0)  23.6 us
    all_to_all x1, waiting for transfers between devices, on_device(): got = lax.all_to_all(sent, 'azi', 0, 0, axis_index_groups=along_x)  15.9 us
    ppermute x1, starting transfers between devices, on_device(): below = lax.ppermute(low, 'rad', [(i + 1, i) for i in range(rad - 1)])  8.12 us
    all_to_all x1, starting transfers between devices, on_device(): got = lax.all_to_all(sent, 'azi', 0, 0, axis_index_groups=along_x)  4.44 us
    ppermute x1, waiting for transfers between devices, on_device(): above = lax.ppermute(high, 'rad', [(i, i + 1) for i in range(rad - 1)])  4.1 us
    pallas_call x1, Pallas kernels, on_device(): call(second_step, f32(16 * PLANES, LANES), [SMEM, SMEM, VMEM], (band, ban...  3.52 us
    unnamed x16, local copies, waits for them, and re-layouts  3.02 us
  transfers between devices with their start and end apart: 3, of which 2 were waited for; matrix products, arithmetic and copies ran while one was open for 0% of the time, Pallas kernels for 0%

profile of v4, /device:TPU:56, one launch (start us, length us, event | category | flops | bytes accessed | tf_op | source)
XLA Modules:
  0.0 103.6 jit_solution(13637471459711187719)
XLA Ops:
  0.0 0.0 copy-start
  0.0 0.9 copy-done
  0.9 8.1 %collective-permute-start = (f32[5,4,6,128]{3,2,1,0:T(8,128)S(1)}, f32[5,4,6,128]{3,2,1,0:T(8,128)S(1)}, u32[]{:S(2)}, u32[]{:S(2)}) collective-permute-start(f32[5,4,6,128]{3,2,1,0:T(8,128)S(1)} %get-tuple-element.24), channel_id=1, source_target_pairs={{16,0},{32,16},{48,32},{64,48},{80,64},{96,80},{112,96},{128,112},... | collective-permute-start | bytes 184328 | tf_op jit(solution)/shard_map/ppermute | solution.py:334
  9.1 1.9 %collective-permute-start.1 = (f32[5,4,6,128]{3,2,1,0:T(8,128)S(1)}, f32[5,4,6,128]{3,2,1,0:T(8,128)S(1)}, u32[]{:S(2)}, u32[]{:S(2)}) collective-permute-start(f32[5,4,6,128]{3,2,1,0:T(8,128)S(1)} %get-tuple-element.25), channel_id=1, source_target_pairs={{0,16},{16,32},{32,48},{48,64},{64,80},{80,96},{96,112},{112,128},... | collective-permute-start | bytes 184328 | tf_op jit(solution)/shard_map/ppermute | solution.py:335
  11.0 0.0 copy-start.1
  11.0 0.7 copy-done.1
  11.7 0.0 copy-start.3
  11.7 0.7 copy-done.3
  12.4 0.0 copy-start.5
  12.4 0.7 copy-done.5
  13.1 0.3 row_values.1.coef_ref
  13.4 0.0 collective-permute-done.below_ref
  13.4 4.1 %collective-permute-done.1.above_ref = f32[5,4,6,128]{3,2,1,0:T(8,128)S(1)} collective-permute-done((f32[5,4,6,128]{3,2,1,0:T(8,128)S(1)}, f32[5,4,6,128]{3,2,1,0:T(8,128)S(1)}, u32[]{:S(2)}, u32[]{:S(2)}) %collective-permute-start.1) | collective-permute-done | bytes 61472 | tf_op jit(solution)/shard_map/ppermute | solution.py:335
  17.5 1.8 %first_step.1 = f32[4,216,128]{2,1,0:T(8,128)S(1)} custom-call(f32[5,4,16,128]{3,2,1,0:T(8,128)S(1)} %get-tuple-element.23.main_ref, f32[5,4,6,128]{3,2,1,0:T(8,128)S(1)} %collective-permute-done.below_ref, f32[5,4,6,128]{3,2,1,0:T(8,128)S(1)} %collective-permute-done.1.above_ref, f32[9,32,128]{2,1,0:T(8,128)S(1)} %row_values.1.coef_ref), custom_call_target="tpu_custom_call" | custom-call | tf_op jit(solution)/shard_map/first_step/pallas_call | solution.py:340
  19.3 34.5 %all_to_all.15.got_ref = f32[4,216,128]{2,1,0:T(8,128)S(1)} all-to-all(f32[4,216,128]{2,1,0:T(8,128)S(1)} %first_step.1), channel_id=1, replica_groups={{0,1,2,3},{4,5,6,7},{8,9,10,11},{12,13,14,15},{16,17,18,19},{20,21,22,2..., dimensions={0} | all-to-all | bytes 884736 | tf_op jit(solution)/shard_map/all_to_all | solution.py:348
  53.8 1.1 %spread.1 = f32[4,592,128]{2,1,0:T(8,128)} custom-call(f32[4,216,128]{2,1,0:T(8,128)S(1)} %all_to_all.15.got_ref), custom_call_target="tpu_custom_call" | custom-call | tf_op jit(solution)/shard_map/spread/pallas_call | solution.py:349
  54.9 0.0 copy-start.4
  54.9 0.0 copy-start.6
  54.9 0.0 copy-start.2
  54.9 0.0 copy-start.7
  54.9 4.4 %all-to-all-start.1 = ((f32[4,592,128]{2,1,0:T(8,128)}), f32[4,592,128]{2,1,0:T(8,128)S(1)}, u32[]{:S(2)}, u32[]{:S(2)}) async-start(f32[4,592,128]{2,1,0:T(8,128)} %spread.1), calls=%async_computation.1 | async-start | bytes 2424832 | tf_op jit(solution)/shard_map/all_to_all | solution.py:376
  59.4 0.0 copy-done.4
  59.4 0.0 copy-done.6
  59.4 0.0 copy-done.2
  59.4 0.1 concatenate.3
  59.5 0.2 copy.12
  59.7 0.0 copy-done.7
  59.7 0.1 pad_dynamic-slice_fusion.1.amount_ref
  59.8 15.9 %all-to-all-done.1 = f32[4,592,128]{2,1,0:T(8,128)S(1)} async-done(((f32[4,592,128]{2,1,0:T(8,128)}), f32[4,592,128]{2,1,0:T(8,128)S(1)}, u32[]{:S(2)}, u32[]{:S(2)}) %all-to-all-start.1) | async-done | bytes 1212448 | tf_op jit(solution)/shard_map/all_to_all | solution.py:376
  75.7 3.5 %second_step.1 = f32[320,128]{1,0:T(8,128)S(1)} custom-call(s32[7]{0:T(128)S(1)} %pad_dynamic-slice_fusion.1.amount_ref, f32[7,9]{1,0:T(8,128)S(1)} %fusion.coef_ref, f32[2368,128]{1,0:T(8,128)S(1)} %bitcast.11), custom_call_target="tpu_custom_call" | custom-call | tf_op jit(solution)/shard_map/second_step/pallas_call | solution.py:378
  79.3 23.6 %all_to_all.16 = f32[16,5,4,128]{3,2,1,0:T(4,128)S(1)} all-to-all(f32[16,5,4,128]{3,2,1,0:T(4,128)S(1)} %bitcast.12), channel_id=1, replica_groups=mesh['rad'=64,'azi'=16] {'azi'}, dimensions={0} | all-to-all | bytes 327680 | tf_op jit(solution)/shard_map/all_to_all | solution.py:381
  102.9 0.7 set_down.1
  (4 shorter events, 0.0 us)
Async XLA Ops:
  0.0 0.9 copy-start
  0.9 12.5 %collective-permute-start = (f32[5,4,6,128]{3,2,1,0:T(8,128)S(1)}, f32[5,4,6,128]{3,2,1,0:T(8,128)S(1)}, u32[]{:S(2)}, u32[]{:S(2)}) collective-permute-start(f32[5,4,6,128]{3,2,1,0:T(8,128)S(1)} %get-tuple-element.24), channel_id=1, source_target_pairs={{16,0},{32,16},{48,32},{64,48},{80,64},{96,80},{112,96},{128,112},... | collective-permute-start | bytes 184328 | tf_op jit(solution)/shard_map/ppermute | solution.py:334
  9.1 8.5 %collective-permute-start.1 = (f32[5,4,6,128]{3,2,1,0:T(8,128)S(1)}, f32[5,4,6,128]{3,2,1,0:T(8,128)S(1)}, u32[]{:S(2)}, u32[]{:S(2)}) collective-permute-start(f32[5,4,6,128]{3,2,1,0:T(8,128)S(1)} %get-tuple-element.25), channel_id=1, source_target_pairs={{0,16},{16,32},{32,48},{48,64},{64,80},{80,96},{96,112},{112,128},... | collective-permute-start | bytes 184328 | tf_op jit(solution)/shard_map/ppermute | solution.py:335
  11.0 0.7 copy-start.1
  11.7 0.7 copy-start.3
  12.4 0.7 copy-start.5
  54.9 4.5 %copy-start.4 = (f32[1024]{0:T(1024)S(1)}, f32[1024]{0:T(1024)}, u32[]{:S(2)}) copy-start(f32[1024]{0:T(1024)} %param.8) | copy-start | bytes 12292
  54.9 4.5 %copy-start.6 = (f32[1024]{0:T(1024)S(1)}, f32[1024]{0:T(1024)}, u32[]{:S(2)}) copy-start(f32[1024]{0:T(1024)} %param.7) | copy-start | bytes 12292
  54.9 4.5 %copy-start.2 = (f32[4,1024]{1,0:T(4,128)S(1)}, f32[4,1024]{1,0:T(4,128)}, u32[]{:S(2)}) copy-start(f32[4,1024]{1,0:T(4,128)} %stiff_hbm) | copy-start | bytes 49156
  54.9 4.8 %copy-start.7 = (s32[1024]{0:T(1024)S(1)}, s32[1024]{0:T(1024)}, u32[]{:S(2)}) copy-start(s32[1024]{0:T(1024)} %param.6) | copy-start | bytes 12292
  54.9 20.8 %all-to-all-start.1 = ((f32[4,592,128]{2,1,0:T(8,128)}), f32[4,592,128]{2,1,0:T(8,128)S(1)}, u32[]{:S(2)}, u32[]{:S(2)}) async-start(f32[4,592,128]{2,1,0:T(8,128)} %spread.1), calls=%async_computation.1 | async-start | bytes 2424832 | tf_op jit(solution)/shard_map/all_to_all | solution.py:376

commit v5 on v4

--- a/solution.py
+++ b/solution.py
@@ -69,42 +69,29 @@
     return start * (1.0 / 3.0) + (2.0 / 3.0) * (now + change)
 
 
-def row_values(
-    spin_hbm, drift_hbm, stiff_hbm, coef_ref, spin_ref, drift_ref, stiff_ref, sems
-):
-    copies = [
-        pltpu.make_async_copy(source, target, sems.at[i])
-        for i, (source, target) in enumerate(
-            ((spin_hbm, spin_ref), (drift_hbm, drift_ref), (stiff_hbm, stiff_ref))
-        )
-    ]
-    for copy in copies:
-        copy.start()
-    for copy in copies:
-        copy.wait()
+def row_values(rows_ref, coef_ref):
     wide = 2 * LANES
-    total = spin_ref.shape[1]
+    total = rows_ref.shape[1]
     row_start = lax.axis_index("rad") * ROWS
     seen = lax.rem(row_start - HALO + total, total)
     here = pl.multiple_of(seen // LANES * LANES, LANES)
     after = pl.multiple_of(lax.rem(here + LANES, total), LANES)
     back = lax.rem(wide - lax.rem(seen, LANES), wide)
-
-    def column(ref, i):
-        pair = [ref[i : i + 1, pl.ds(start, LANES)] for start in (here, after)]
-        pair = jnp.concatenate(pair, axis=1)
-        pair = jnp.broadcast_to(pair, (8, wide))
-        tall = jnp.transpose(pltpu.roll(pair, back, 1)[:, 0:LANES])[0:TALL]
-        tall = pltpu.roll(tall, TALL - HALO, 0)
-        return jnp.broadcast_to(tall[:, 0:1], (TALL, LANES))
-
-    spin, drift = column(spin_ref, 0), column(drift_ref, 0)
+    pair = [rows_ref[:, pl.ds(start, LANES)] for start in (here, after)]
+    pair = pltpu.roll(jnp.concatenate(pair, axis=1), back, 1)
+    tall = jnp.transpose(pair[:, 0:LANES])[0:TALL]
+    tall = pltpu.roll(tall, TALL - HALO, 0)
+
+    def column(i):
+        return jnp.broadcast_to(tall[:, i : i + 1], (TALL, LANES))
+
+    spin, drift = column(0), column(1)
     coef_ref[0] = NEAR - HD * drift
     coef_ref[1] = NEAR + HD * drift
     coef_ref[2] = (2.0 * DT) * spin
     coef_ref[3] = (0.5 * DT) * spin
     for k in range(LEVELS):
-        coef_ref[4 + k] = column(stiff_ref, k)
+        coef_ref[4 + k] = column(2 + k)
     local = lax.broadcasted_iota(jnp.int32, (TALL, LANES), 0)
     local = row_start + jnp.where(local < ROWS + HALO, local, local - TALL)
     inside = (local >= 0) & (local < total)
@@ -116,12 +103,10 @@
     below_ref,
     above_ref,
     coef_ref,
-    send_ref,
-    begin,
-    one,
-    two,
-    table,
+    *rest,
 ):
+    send_refs = rest[0:4]
+    begin, one, two, table, ordered = rest[4:]
     wide = 2 * LANES
     for plane in range(PLANES):
         f, k = divmod(plane, LEVELS)
@@ -181,19 +166,26 @@
                     spill = jnp.where(mine, past, spill)
     table[pl.ds(PLANES, PACK, HELD), :] = pltpu.roll(spill, REACH, 0)[0:PACK]
     size = (4 + HALO) * HELD
+    place = lax.axis_index("azi") % 4
     for group in range(4):
-        send_ref[group, 0:size, :] = table[group * 4 * HELD : group * 4 * HELD + size]
-        send_ref[group, size:, :] = jnp.zeros(
-            (send_ref.shape[1] - size, LANES), jnp.float32
+        ordered[group, 0:size, :] = table[group * 4 * HELD : group * 4 * HELD + size]
+        ordered[group, size:, :] = jnp.zeros(
+            (ordered.shape[1] - size, LANES), jnp.float32
         )
-
-
-def spread(got_ref, send_ref):
+    for distance in range(4):
+        send_refs[distance][...] = ordered[(place + distance) % 4]
+
+
+def spread(*refs):
+    got_refs, send_ref, ordered = refs[0:4], refs[4], refs[5]
     size = (1 + HALO) * HELD
+    place = lax.axis_index("azi") % 4
+    for distance in range(4):
+        ordered[(place + 4 - distance) % 4] = got_refs[distance][...]
     for target in range(4):
         for z in range(4):
             start = z * BAND
-            send_ref[target, start : start + size, :] = got_ref[
+            send_ref[target, start : start + size, :] = ordered[
                 z, target * HELD : target * HELD + size, :
             ]
             send_ref[target, start + size : start + BAND, :] = jnp.zeros(
@@ -317,20 +309,10 @@
 
     few = f32(FIELDS, LEVELS, HALO, LANES)
     low, high, state = call(cut, (few, few, f32(*state.shape)), [VMEM])(state)
-    spin, drift, stiffness, low, high = lax.optimization_barrier(
-        (spin, drift, stiffness, low, high)
-    )
-    coefs = call(
-        row_values,
-        f32(5 + LEVELS, TALL, LANES),
-        [pl.BlockSpec(memory_space=pltpu.HBM)] * 3,
-        (
-            pltpu.VMEM((1, total), jnp.float32),
-            pltpu.VMEM((1, total), jnp.float32),
-            pltpu.VMEM((LEVELS, total), jnp.float32),
-            pltpu.SemaphoreType.DMA((3,)),
-        ),
-    )(spin[None], drift[None], stiffness)
+    named = [spin[None], drift[None], stiffness]
+    coefs = call(row_values, f32(5 + LEVELS, TALL, LANES), [VMEM])(
+        jnp.concatenate(named + named[0:2], axis=0)
+    )
     below = lax.ppermute(low, "rad", [(i + 1, i) for i in range(rad - 1)])
     above = lax.ppermute(high, "rad", [(i, i + 1) for i in range(rad - 1)])
 
@@ -339,14 +321,31 @@
     tile = pltpu.VMEM((PLANES, TALL, 2 * LANES), jnp.float32)
     sent = call(
         first_step,
-        f32(4, count, LANES),
+        (f32(count, LANES),) * 4,
         [VMEM] * 4,
-        (tile, tile, tile, pltpu.VMEM((PACK * HELD, LANES), jnp.float32)),
+        (
+            tile,
+            tile,
+            tile,
+            pltpu.VMEM((PACK * HELD, LANES), jnp.float32),
+            pltpu.VMEM((4, count, LANES), jnp.float32),
+        ),
     )(state, below, above, coefs)
-    along_z = [[4 * x + z for z in range(4)] for x in range(4)]
     along_x = [[4 * x + z for x in range(4)] for z in range(4)]
-    got = lax.all_to_all(sent, "azi", 0, 0, axis_index_groups=along_z)
-    sent = call(spread, f32(4, 4 * BAND, LANES), [VMEM])(got)
+    far, ahead, back = (
+        lax.ppermute(
+            sent[distance],
+            "azi",
+            [(4 * x + z, 4 * x + (z + distance) % 4) for x in range(4) for z in range(4)],
+        )
+        for distance in (2, 1, 3)
+    )
+    sent = call(
+        spread,
+        f32(4, 4 * BAND, LANES),
+        [VMEM] * 4,
+        (pltpu.VMEM((4, count, LANES), jnp.float32),),
+    )(sent[0], ahead, far, back)
 
     spin, drift, stiffness, shifts, sent = lax.optimization_barrier(
         (spin, drift, stiffness, shifts, sent)

time: 105 us -> 107 us (1.019); the launches traced: 104 us -> 107 us
  blocking collectives: 58.1 us -> 24.3 us
  starting transfers between devices: 14.5 us -> 40.9 us
  waiting for transfers between devices: 20 us -> 31.8 us
  local copies, waits for them, and re-layouts: 3.39 us -> 2.12 us
    all_to_all x1 -> x0, blocking collectives: 34.5 us -> none  [on_device(): got = lax.all_to_all(sent, 'azi', 0, 0, axis_index_groups=along_z)]
    ppermute x0 -> x3, starting transfers between devices: none -> 26.4 us  [on_device(): lax.ppermute(sent[distance], 'azi', [(4 * x + z, 4 * x + (z + distance) %...]
    ppermute x0 -> x3, waiting for transfers between devices: none -> 9.9 us  [on_device(): lax.ppermute(sent[distance], 'azi', [(4 * x + z, 4 * x + (z + distance) %...]
    unnamed x16 -> x10, local copies, waits for them, and re-layouts: 3.02 us -> 0.93 us
    ppermute x1, waiting for transfers between devices: 4.1 us -> 5.44 us  [on_device(): above = lax.ppermute(high, 'rad', [(i, i + 1) for i in range(rad - 1)])]
  transfers between devices with their start and end apart: 3 -> 6, of which waited for: 2 -> 4; matrix products, arithmetic and copies ran while one was open for 0% -> 1% of each run, Pallas kernels for 0% -> 0%
where the time goes in v5:
time: 107 us
  starting transfers between devices  40.9 us (38%)
  waiting for transfers between devices  31.8 us (30%)
  blocking collectives  24.3 us (23%)
  Pallas kernels  7.5 us (7%)
  local copies, waits for them, and re-layouts  2.12 us (2%)
    ppermute x3, starting transfers between devices, on_device(): lax.ppermute(sent[distance], 'azi', [(4 * x + z, 4 * x + (z + distance) %...  26.4 us
    all_to_all x1, blocking collectives, on_device(): got = lax.all_to_all(sent.reshape(16, FIELDS, LEVELS, LANES), 'azi', 0, 0)  24.3 us
    all_to_all x1, waiting for transfers between devices, on_device(): got = lax.all_to_all(sent, 'azi', 0, 0, axis_index_groups=along_x)  16.5 us
    ppermute x3, waiting for transfers between devices, on_device(): lax.ppermute(sent[distance], 'azi', [(4 * x + z, 4 * x + (z + distance) %...  9.9 us
    ppermute x1, starting transfers between devices, on_device(): below = lax.ppermute(low, 'rad', [(i + 1, i) for i in range(rad - 1)])  8.12 us
    ppermute x1, waiting for transfers between devices, on_device(): above = lax.ppermute(high, 'rad', [(i, i + 1) for i in range(rad - 1)])  5.44 us
    all_to_all x1, starting transfers between devices, on_device(): got = lax.all_to_all(sent, 'azi', 0, 0, axis_index_groups=along_x)  4.44 us
    pallas_call x1, Pallas kernels, on_device(): call(second_step, f32(16 * PLANES, LANES), [SMEM, SMEM, VMEM], (band, ban...  3.52 us
  transfers between devices with their start and end apart: 6, of which 4 were waited for; matrix products, arithmetic and copies ran while one was open for 1% of the time, Pallas kernels for 0%

profile of v5, /device:TPU:56, one launch (start us, length us, event | category | flops | bytes accessed | tf_op | source)
XLA Modules:
  0.0 106.8 jit_solution(12870195362241442014)
XLA Ops:
  0.0 0.0 copy-start
  0.0 0.9 copy-done
  0.9 8.1 %collective-permute-start = (f32[5,4,6,128]{3,2,1,0:T(8,128)S(1)}, f32[5,4,6,128]{3,2,1,0:T(8,128)S(1)}, u32[]{:S(2)}, u32[]{:S(2)}) collective-permute-start(f32[5,4,6,128]{3,2,1,0:T(8,128)S(1)} %get-tuple-element.18), channel_id=1, source_target_pairs={{16,0},{32,16},{48,32},{64,48},{80,64},{96,80},{112,96},{128,112},... | collective-permute-start | bytes 184328 | tf_op jit(solution)/shard_map/ppermute | solution.py:316
  9.1 1.9 %collective-permute-start.1 = (f32[5,4,6,128]{3,2,1,0:T(8,128)S(1)}, f32[5,4,6,128]{3,2,1,0:T(8,128)S(1)}, u32[]{:S(2)}, u32[]{:S(2)}) collective-permute-start(f32[5,4,6,128]{3,2,1,0:T(8,128)S(1)} %get-tuple-element.19), channel_id=1, source_target_pairs={{0,16},{16,32},{32,48},{48,64},{64,80},{80,96},{96,112},{112,128},... | collective-permute-start | bytes 184328 | tf_op jit(solution)/shard_map/ppermute | solution.py:317
  11.0 0.8 concatenate.6.rows_ref
  11.8 0.3 row_values.1.coef_ref
  12.1 0.0 collective-permute-done.below_ref
  12.1 5.4 %collective-permute-done.1.above_ref = f32[5,4,6,128]{3,2,1,0:T(8,128)S(1)} collective-permute-done((f32[5,4,6,128]{3,2,1,0:T(8,128)S(1)}, f32[5,4,6,128]{3,2,1,0:T(8,128)S(1)}, u32[]{:S(2)}, u32[]{:S(2)}) %collective-permute-start.1) | collective-permute-done | bytes 61472 | tf_op jit(solution)/shard_map/ppermute | solution.py:317
  17.5 1.8 %first_step.1 = (f32[216,128]{1,0:T(8,128)S(1)}, f32[216,128]{1,0:T(8,128)S(1)}, f32[216,128]{1,0:T(8,128)S(1)}, f32[216,128]{1,0:T(8,128)S(1)}) custom-call(f32[5,4,16,128]{3,2,1,0:T(8,128)S(1)} %get-tuple-element.17.main_ref, f32[5,4,6,128]{3,2,1,0:T(8,128)S(1)} %collective-permute-done.below_ref, f32[5,4,6,128]{3,2,1,0:T(8,128)S(1)} %collective-permute-done.1.above_ref, ...), custom_call_target="tpu_custom_call" | custom-call | tf_op jit(solution)/shard_map/first_step/pallas_call | solution.py:322
  19.3 10.9 %collective-permute-start.2 = (f32[216,128]{1,0:T(8,128)S(1)}, f32[216,128]{1,0:T(8,128)S(1)}, u32[]{:S(2)}, u32[]{:S(2)}) collective-permute-start(f32[216,128]{1,0:T(8,128)S(1)} %get-tuple-element.21), channel_id=1, source_target_pairs={{0,1},{1,2},{2,3},{3,0},{4,5},{5,6},{6,7},{7,4},{8,9},{9,10},{10,1... | collective-permute-start | bytes 331784 | tf_op jit(solution)/shard_map/ppermute | solution.py:336
  30.3 11.9 %collective-permute-start.3 = (f32[216,128]{1,0:T(8,128)S(1)}, f32[216,128]{1,0:T(8,128)S(1)}, u32[]{:S(2)}, u32[]{:S(2)}) collective-permute-start(f32[216,128]{1,0:T(8,128)S(1)} %get-tuple-element.22), channel_id=1, source_target_pairs={{0,2},{1,3},{2,0},{3,1},{4,6},{5,7},{6,4},{7,5},{8,10},{9,11},{10,... | collective-permute-start | bytes 331784 | tf_op jit(solution)/shard_map/ppermute | solution.py:336
  42.1 3.6 %collective-permute-start.4 = (f32[216,128]{1,0:T(8,128)S(1)}, f32[216,128]{1,0:T(8,128)S(1)}, u32[]{:S(2)}, u32[]{:S(2)}) collective-permute-start(f32[216,128]{1,0:T(8,128)S(1)} %get-tuple-element.23), channel_id=1, source_target_pairs={{0,3},{1,0},{2,1},{3,2},{4,7},{5,4},{6,5},{7,6},{8,11},{9,8},{10,9... | collective-permute-start | bytes 331784 | tf_op jit(solution)/shard_map/ppermute | solution.py:336
  45.8 0.0 collective-permute-done.2.refs_1_
  45.8 4.0 %collective-permute-done.3.refs_2_ = f32[216,128]{1,0:T(8,128)S(1)} collective-permute-done((f32[216,128]{1,0:T(8,128)S(1)}, f32[216,128]{1,0:T(8,128)S(1)}, u32[]{:S(2)}, u32[]{:S(2)}) %collective-permute-start.3) | collective-permute-done | bytes 110624 | tf_op jit(solution)/shard_map/ppermute | solution.py:336
  49.8 5.9 %collective-permute-done.4.refs_3_ = f32[216,128]{1,0:T(8,128)S(1)} collective-permute-done((f32[216,128]{1,0:T(8,128)S(1)}, f32[216,128]{1,0:T(8,128)S(1)}, u32[]{:S(2)}, u32[]{:S(2)}) %collective-permute-start.4) | collective-permute-done | bytes 110624 | tf_op jit(solution)/shard_map/ppermute | solution.py:336
  55.7 1.2 %spread.1 = f32[4,592,128]{2,1,0:T(8,128)} custom-call(f32[216,128]{1,0:T(8,128)S(1)} %get-tuple-element.20.refs_0_, f32[216,128]{1,0:T(8,128)S(1)} %collective-permute-done.2.refs_1_, f32[216,128]{1,0:T(8,128)S(1)} %collective-permute-done.3.refs_2_, f32[216,128]{1,0:T(8,128)S(1)} %collective-permute-done.4.refs_3_), custom_call_target="tpu_custom_call" | custom-call | tf_op jit(solution)/shard_map/spread/pallas_call | solution.py:343
  56.9 0.0 copy-start.2
  56.9 0.0 copy-start.3
  56.9 0.0 copy-start.1
  56.9 0.0 copy-start.4
  56.9 4.4 %all-to-all-start = ((f32[4,592,128]{2,1,0:T(8,128)}), f32[4,592,128]{2,1,0:T(8,128)S(1)}, u32[]{:S(2)}, u32[]{:S(2)}) async-start(f32[4,592,128]{2,1,0:T(8,128)} %spread.1), calls=%async_computation | async-start | bytes 2424832 | tf_op jit(solution)/shard_map/all_to_all | solution.py:375
  61.3 0.0 copy-done.2
  61.3 0.0 copy-done.3
  61.3 0.0 copy-done.1
  61.3 0.1 concatenate.7
  61.4 0.2 copy.12
  61.6 0.0 copy-done.4
  61.6 0.1 pad_dynamic-slice_fusion.1.amount_ref
  61.7 16.5 %all-to-all-done = f32[4,592,128]{2,1,0:T(8,128)S(1)} async-done(((f32[4,592,128]{2,1,0:T(8,128)}), f32[4,592,128]{2,1,0:T(8,128)S(1)}, u32[]{:S(2)}, u32[]{:S(2)}) %all-to-all-start) | async-done | bytes 1212448 | tf_op jit(solution)/shard_map/all_to_all | solution.py:375
  78.2 3.5 %second_step.1 = f32[320,128]{1,0:T(8,128)S(1)} custom-call(s32[7]{0:T(128)S(1)} %pad_dynamic-slice_fusion.1.amount_ref, f32[7,9]{1,0:T(8,128)S(1)} %fusion.coef_ref, f32[2368,128]{1,0:T(8,128)S(1)} %bitcast.11), custom_call_target="tpu_custom_call" | custom-call | tf_op jit(solution)/shard_map/second_step/pallas_call | solution.py:377
  81.8 24.3 %all_to_all.10 = f32[16,5,4,128]{3,2,1,0:T(4,128)S(1)} all-to-all(f32[16,5,4,128]{3,2,1,0:T(4,128)S(1)} %bitcast.12), channel_id=1, replica_groups=mesh['rad'=64,'azi'=16] {'azi'}, dimensions={0} | all-to-all | bytes 327680 | tf_op jit(solution)/shard_map/all_to_all | solution.py:380
  106.1 0.7 set_down.1
  (4 shorter events, 0.0 us)
Async XLA Ops:
  0.0 0.9 copy-start
  0.9 11.1 %collective-permute-start = (f32[5,4,6,128]{3,2,1,0:T(8,128)S(1)}, f32[5,4,6,128]{3,2,1,0:T(8,128)S(1)}, u32[]{:S(2)}, u32[]{:S(2)}) collective-permute-start(f32[5,4,6,128]{3,2,1,0:T(8,128)S(1)} %get-tuple-element.18), channel_id=1, source_target_pairs={{16,0},{32,16},{48,32},{64,48},{80,64},{96,80},{112,96},{128,112},... | collective-permute-start | bytes 184328 | tf_op jit(solution)/shard_map/ppermute | solution.py:316
  9.1 8.5 %collective-permute-start.1 = (f32[5,4,6,128]{3,2,1,0:T(8,128)S(1)}, f32[5,4,6,128]{3,2,1,0:T(8,128)S(1)}, u32[]{:S(2)}, u32[]{:S(2)}) collective-permute-start(f32[5,4,6,128]{3,2,1,0:T(8,128)S(1)} %get-tuple-element.19), channel_id=1, source_target_pairs={{0,16},{16,32},{32,48},{48,64},{64,80},{80,96},{96,112},{112,128},... | collective-permute-start | bytes 184328 | tf_op jit(solution)/shard_map/ppermute | solution.py:317
  19.3 26.4 %collective-permute-start.2 = (f32[216,128]{1,0:T(8,128)S(1)}, f32[216,128]{1,0:T(8,128)S(1)}, u32[]{:S(2)}, u32[]{:S(2)}) collective-permute-start(f32[216,128]{1,0:T(8,128)S(1)} %get-tuple-element.21), channel_id=1, source_target_pairs={{0,1},{1,2},{2,3},{3,0},{4,5},{5,6},{6,7},{7,4},{8,9},{9,10},{10,1... | collective-permute-start | bytes 331784 | tf_op jit(solution)/shard_map/ppermute | solution.py:336
  30.3 19.5 %collective-permute-start.3 = (f32[216,128]{1,0:T(8,128)S(1)}, f32[216,128]{1,0:T(8,128)S(1)}, u32[]{:S(2)}, u32[]{:S(2)}) collective-permute-start(f32[216,128]{1,0:T(8,128)S(1)} %get-tuple-element.22), channel_id=1, source_target_pairs={{0,2},{1,3},{2,0},{3,1},{4,6},{5,7},{6,4},{7,5},{8,10},{9,11},{10,... | collective-permute-start | bytes 331784 | tf_op jit(solution)/shard_map/ppermute | solution.py:336
  42.1 13.6 %collective-permute-start.4 = (f32[216,128]{1,0:T(8,128)S(1)}, f32[216,128]{1,0:T(8,128)S(1)}, u32[]{:S(2)}, u32[]{:S(2)}) collective-permute-start(f32[216,128]{1,0:T(8,128)S(1)} %get-tuple-element.23), channel_id=1, source_target_pairs={{0,3},{1,0},{2,1},{3,2},{4,7},{5,4},{6,5},{7,6},{8,11},{9,8},{10,9... | collective-permute-start | bytes 331784 | tf_op jit(solution)/shard_map/ppermute | solution.py:336
  56.9 4.5 %copy-start.2 = (f32[1024]{0:T(1024)S(1)}, f32[1024]{0:T(1024)}, u32[]{:S(2)}) copy-start(f32[1024]{0:T(1024)} %param.8) | copy-start | bytes 12292
  56.9 4.5 %copy-start.3 = (f32[1024]{0:T(1024)S(1)}, f32[1024]{0:T(1024)}, u32[]{:S(2)}) copy-start(f32[1024]{0:T(1024)} %param.7) | copy-start | bytes 12292
  56.9 4.5 %copy-start.1 = (f32[4,1024]{1,0:T(4,128)S(1)}, f32[4,1024]{1,0:T(4,128)}, u32[]{:S(2)}) copy-start(f32[4,1024]{1,0:T(4,128)} %param.9) | copy-start | bytes 49156
  56.9 4.8 %copy-start.4 = (s32[1024]{0:T(1024)S(1)}, s32[1024]{0:T(1024)}, u32[]{:S(2)}) copy-start(s32[1024]{0:T(1024)} %param.6) | copy-start | bytes 12292
  56.9 21.4 %all-to-all-start = ((f32[4,592,128]{2,1,0:T(8,128)}), f32[4,592,128]{2,1,0:T(8,128)S(1)}, u32[]{:S(2)}, u32[]{:S(2)}) async-start(f32[4,592,128]{2,1,0:T(8,128)} %spread.1), calls=%async_computation | async-start | bytes 2424832 | tf_op jit(solution)/shard_map/all_to_all | solution.py:375

commit v6 on v4

--- a/solution.py
+++ b/solution.py
@@ -69,42 +69,29 @@
     return start * (1.0 / 3.0) + (2.0 / 3.0) * (now + change)
 
 
-def row_values(
-    spin_hbm, drift_hbm, stiff_hbm, coef_ref, spin_ref, drift_ref, stiff_ref, sems
-):
-    copies = [
-        pltpu.make_async_copy(source, target, sems.at[i])
-        for i, (source, target) in enumerate(
-            ((spin_hbm, spin_ref), (drift_hbm, drift_ref), (stiff_hbm, stiff_ref))
-        )
-    ]
-    for copy in copies:
-        copy.start()
-    for copy in copies:
-        copy.wait()
+def row_values(rows_ref, coef_ref):
     wide = 2 * LANES
-    total = spin_ref.shape[1]
+    total = rows_ref.shape[1]
     row_start = lax.axis_index("rad") * ROWS
     seen = lax.rem(row_start - HALO + total, total)
     here = pl.multiple_of(seen // LANES * LANES, LANES)
     after = pl.multiple_of(lax.rem(here + LANES, total), LANES)
     back = lax.rem(wide - lax.rem(seen, LANES), wide)
-
-    def column(ref, i):
-        pair = [ref[i : i + 1, pl.ds(start, LANES)] for start in (here, after)]
-        pair = jnp.concatenate(pair, axis=1)
-        pair = jnp.broadcast_to(pair, (8, wide))
-        tall = jnp.transpose(pltpu.roll(pair, back, 1)[:, 0:LANES])[0:TALL]
-        tall = pltpu.roll(tall, TALL - HALO, 0)
-        return jnp.broadcast_to(tall[:, 0:1], (TALL, LANES))
-
-    spin, drift = column(spin_ref, 0), column(drift_ref, 0)
+    pair = [rows_ref[:, pl.ds(start, LANES)] for start in (here, after)]
+    pair = pltpu.roll(jnp.concatenate(pair, axis=1), back, 1)
+    tall = jnp.transpose(pair[:, 0:LANES])[0:TALL]
+    tall = pltpu.roll(tall, TALL - HALO, 0)
+
+    def column(i):
+        return jnp.broadcast_to(tall[:, i : i + 1], (TALL, LANES))
+
+    spin, drift = column(0), column(1)
     coef_ref[0] = NEAR - HD * drift
     coef_ref[1] = NEAR + HD * drift
     coef_ref[2] = (2.0 * DT) * spin
     coef_ref[3] = (0.5 * DT) * spin
     for k in range(LEVELS):
-        coef_ref[4 + k] = column(stiff_ref, k)
+        coef_ref[4 + k] = column(2 + k)
     local = lax.broadcasted_iota(jnp.int32, (TALL, LANES), 0)
     local = row_start + jnp.where(local < ROWS + HALO, local, local - TALL)
     inside = (local >= 0) & (local < total)
@@ -238,7 +225,7 @@
     for stage in range(3):
         src, dst = sources[stage], targets[stage]
 
-        def section(row, carry, stage=stage, src=src, dst=dst):
+        def section(row):
             scalars = [coef_ref[row, i] for i in range(5 + LEVELS)]
             inside = scalars[4 + LEVELS] > 0.5
             for k in range(LEVELS):
@@ -266,17 +253,16 @@
                     plane = f * LEVELS + k
                     value = combine(stage, begin[row, plane], src[row, plane], change[f])
                     if dst is not None:
-                        dst[row, plane] = jnp.where(inside, value, 0.0)
+                        if row != REACH:
+                            value = jnp.where(inside, value, 0.0)
+                        dst[row, plane] = value
                     else:
                         send_ref[pl.ds(plane, 16, PLANES), :] = turned(
                             value, last_amount, lane
                         )
-            return carry
-
-        if dst is not None:
-            lax.fori_loop(stage + 1, span - 1 - stage, section, 0)
-        else:
-            section(REACH, 0)
+
+        for row in range(stage + 1, span - 1 - stage):
+            section(row)
 
 
 def set_down(got_ref, out_ref):
@@ -317,20 +303,10 @@
 
     few = f32(FIELDS, LEVELS, HALO, LANES)
     low, high, state = call(cut, (few, few, f32(*state.shape)), [VMEM])(state)
-    spin, drift, stiffness, low, high = lax.optimization_barrier(
-        (spin, drift, stiffness, low, high)
-    )
-    coefs = call(
-        row_values,
-        f32(5 + LEVELS, TALL, LANES),
-        [pl.BlockSpec(memory_space=pltpu.HBM)] * 3,
-        (
-            pltpu.VMEM((1, total), jnp.float32),
-            pltpu.VMEM((1, total), jnp.float32),
-            pltpu.VMEM((LEVELS, total), jnp.float32),
-            pltpu.SemaphoreType.DMA((3,)),
-        ),
-    )(spin[None], drift[None], stiffness)
+    named = [spin[None], drift[None], stiffness]
+    coefs = call(row_values, f32(5 + LEVELS, TALL, LANES), [VMEM])(
+        jnp.concatenate(named + named[0:2], axis=0)
+    )
     below = lax.ppermute(low, "rad", [(i + 1, i) for i in range(rad - 1)])
     above = lax.ppermute(high, "rad", [(i, i + 1) for i in range(rad - 1)])
 

time: 105 us -> 104 us (level); the launches traced: 104 us -> 104 us
  blocking collectives: 58.1 us -> 61 us
  local copies, waits for them, and re-layouts: 3.39 us -> 2.12 us
    all_to_all x1, waiting for transfers between devices: 15.9 us -> 13.5 us  [on_device(): got = lax.all_to_all(sent, 'azi', 0, 0, axis_index_groups=along_x)]
    all_to_all x1, blocking collectives: 34.5 us -> 36.7 us  [on_device(): got = lax.all_to_all(sent, 'azi', 0, 0, axis_index_groups=along_z)]
    unnamed x16 -> x10, local copies, waits for them, and re-layouts: 3.02 us -> 0.93 us
    ppermute x1, waiting for transfers between devices: 4.1 us -> 5.44 us  [on_device(): above = lax.ppermute(high, 'rad', [(i, i + 1) for i in range(rad - 1)])]
  transfers between devices with their start and end apart: 3 -> 3, of which waited for: 2 -> 2; matrix products, arithmetic and copies ran while one was open for 0% -> 1% of each run, Pallas kernels for 0% -> 0%
where the time goes in v6:
time: 104 us
  blocking collectives  61 us (59%)
  waiting for transfers between devices  19 us (18%)
  starting transfers between devices  14.5 us (14%)
  Pallas kernels  7.02 us (7%)
  local copies, waits for them, and re-layouts  2.12 us (2%)
    all_to_all x1, blocking collectives, on_device(): got = lax.all_to_all(sent, 'azi', 0, 0, axis_index_groups=along_z)  36.7 us
    all_to_all x1, blocking collectives, on_device(): got = lax.all_to_all(sent.reshape(16, FIELDS, LEVELS, LANES), 'azi', 0, 0)  24.3 us
    all_to_all x1, waiting for transfers between devices, on_device(): got = lax.all_to_all(sent, 'azi', 0, 0, axis_index_groups=along_x)  13.5 us
    ppermute x1, starting transfers between devices, on_device(): below = lax.ppermute(low, 'rad', [(i + 1, i) for i in range(rad - 1)])  8.12 us
    ppermute x1, waiting for transfers between devices, on_device(): above = lax.ppermute(high, 'rad', [(i, i + 1) for i in range(rad - 1)])  5.44 us
    all_to_all x1, starting transfers between devices, on_device(): got = lax.all_to_all(sent, 'azi', 0, 0, axis_index_groups=along_x)  4.44 us
    pallas_call x1, Pallas kernels, on_device(): call(second_step, f32(16 * PLANES, LANES), [SMEM, SMEM, VMEM], (band, ban...  3.11 us
  transfers between devices with their start and end apart: 3, of which 2 were waited for; matrix products, arithmetic and copies ran while one was open for 1% of the time, Pallas kernels for 0%

profile of v6, /device:TPU:56, one launch (start us, length us, event | category | flops | bytes accessed | tf_op | source)
XLA Modules:
  0.0 103.7 jit_solution(13256136181316541500)
XLA Ops:
  0.0 0.0 copy-start
  0.0 0.9 copy-done
  0.9 8.1 %collective-permute-start = (f32[5,4,6,128]{3,2,1,0:T(8,128)S(1)}, f32[5,4,6,128]{3,2,1,0:T(8,128)S(1)}, u32[]{:S(2)}, u32[]{:S(2)}) collective-permute-start(f32[5,4,6,128]{3,2,1,0:T(8,128)S(1)} %get-tuple-element.14), channel_id=1, source_target_pairs={{16,0},{32,16},{48,32},{64,48},{80,64},{96,80},{112,96},{128,112},... | collective-permute-start | bytes 184328 | tf_op jit(solution)/shard_map/ppermute | solution.py:310
  9.1 1.9 %collective-permute-start.1 = (f32[5,4,6,128]{3,2,1,0:T(8,128)S(1)}, f32[5,4,6,128]{3,2,1,0:T(8,128)S(1)}, u32[]{:S(2)}, u32[]{:S(2)}) collective-permute-start(f32[5,4,6,128]{3,2,1,0:T(8,128)S(1)} %get-tuple-element.15), channel_id=1, source_target_pairs={{0,16},{16,32},{32,48},{48,64},{64,80},{80,96},{96,112},{112,128},... | collective-permute-start | bytes 184328 | tf_op jit(solution)/shard_map/ppermute | solution.py:311
  11.0 0.8 concatenate.6.rows_ref
  11.8 0.3 row_values.1.coef_ref
  12.1 0.0 collective-permute-done.below_ref
  12.1 5.4 %collective-permute-done.1.above_ref = f32[5,4,6,128]{3,2,1,0:T(8,128)S(1)} collective-permute-done((f32[5,4,6,128]{3,2,1,0:T(8,128)S(1)}, f32[5,4,6,128]{3,2,1,0:T(8,128)S(1)}, u32[]{:S(2)}, u32[]{:S(2)}) %collective-permute-start.1) | collective-permute-done | bytes 61472 | tf_op jit(solution)/shard_map/ppermute | solution.py:311
  17.5 1.8 %first_step.1 = f32[4,216,128]{2,1,0:T(8,128)S(1)} custom-call(f32[5,4,16,128]{3,2,1,0:T(8,128)S(1)} %get-tuple-element.13.main_ref, f32[5,4,6,128]{3,2,1,0:T(8,128)S(1)} %collective-permute-done.below_ref, f32[5,4,6,128]{3,2,1,0:T(8,128)S(1)} %collective-permute-done.1.above_ref, f32[9,32,128]{2,1,0:T(8,128)S(1)} %row_values.1.coef_ref), custom_call_target="tpu_custom_call" | custom-call | tf_op jit(solution)/shard_map/first_step/pallas_call | solution.py:316
  19.3 36.7 %all_to_all.15.got_ref = f32[4,216,128]{2,1,0:T(8,128)S(1)} all-to-all(f32[4,216,128]{2,1,0:T(8,128)S(1)} %first_step.1), channel_id=1, replica_groups={{0,1,2,3},{4,5,6,7},{8,9,10,11},{12,13,14,15},{16,17,18,19},{20,21,22,2..., dimensions={0} | all-to-all | bytes 884736 | tf_op jit(solution)/shard_map/all_to_all | solution.py:324
  56.0 1.1 %spread.1 = f32[4,592,128]{2,1,0:T(8,128)} custom-call(f32[4,216,128]{2,1,0:T(8,128)S(1)} %all_to_all.15.got_ref), custom_call_target="tpu_custom_call" | custom-call | tf_op jit(solution)/shard_map/spread/pallas_call | solution.py:325
  57.1 0.0 copy-start.2
  57.1 0.0 copy-start.3
  57.1 0.0 copy-start.1
  57.1 0.0 copy-start.4
  57.1 4.4 %all-to-all-start.1 = ((f32[4,592,128]{2,1,0:T(8,128)}), f32[4,592,128]{2,1,0:T(8,128)S(1)}, u32[]{:S(2)}, u32[]{:S(2)}) async-start(f32[4,592,128]{2,1,0:T(8,128)} %spread.1), calls=%async_computation.1 | async-start | bytes 2424832 | tf_op jit(solution)/shard_map/all_to_all | solution.py:352
  61.6 0.0 copy-done.2
  61.6 0.0 copy-done.3
  61.6 0.0 copy-done.1
  61.6 0.1 concatenate.7
  61.7 0.2 copy.12
  61.9 0.0 copy-done.4
  61.9 0.1 pad_dynamic-slice_fusion.1.amount_ref
  62.0 13.5 %all-to-all-done.1 = f32[4,592,128]{2,1,0:T(8,128)S(1)} async-done(((f32[4,592,128]{2,1,0:T(8,128)}), f32[4,592,128]{2,1,0:T(8,128)S(1)}, u32[]{:S(2)}, u32[]{:S(2)}) %all-to-all-start.1) | async-done | bytes 1212448 | tf_op jit(solution)/shard_map/all_to_all | solution.py:352
  75.6 3.1 %second_step.1 = f32[320,128]{1,0:T(8,128)S(1)} custom-call(s32[7]{0:T(128)S(1)} %pad_dynamic-slice_fusion.1.amount_ref, f32[7,9]{1,0:T(8,128)S(1)} %fusion.coef_ref, f32[2368,128]{1,0:T(8,128)S(1)} %bitcast.11), custom_call_target="tpu_custom_call" | custom-call | tf_op jit(solution)/shard_map/second_step/pallas_call | solution.py:354
  78.7 24.3 %all_to_all.16 = f32[16,5,4,128]{3,2,1,0:T(4,128)S(1)} all-to-all(f32[16,5,4,128]{3,2,1,0:T(4,128)S(1)} %bitcast.12), channel_id=1, replica_groups=mesh['rad'=64,'azi'=16] {'azi'}, dimensions={0} | all-to-all | bytes 327680 | tf_op jit(solution)/shard_map/all_to_all | solution.py:357
  102.9 0.7 set_down.1
  (4 shorter events, 0.0 us)
Async XLA Ops:
  0.0 0.9 copy-start
  0.9 11.1 %collective-permute-start = (f32[5,4,6,128]{3,2,1,0:T(8,128)S(1)}, f32[5,4,6,128]{3,2,1,0:T(8,128)S(1)}, u32[]{:S(2)}, u32[]{:S(2)}) collective-permute-start(f32[5,4,6,128]{3,2,1,0:T(8,128)S(1)} %get-tuple-element.14), channel_id=1, source_target_pairs={{16,0},{32,16},{48,32},{64,48},{80,64},{96,80},{112,96},{128,112},... | collective-permute-start | bytes 184328 | tf_op jit(solution)/shard_map/ppermute | solution.py:310
  9.1 8.5 %collective-permute-start.1 = (f32[5,4,6,128]{3,2,1,0:T(8,128)S(1)}, f32[5,4,6,128]{3,2,1,0:T(8,128)S(1)}, u32[]{:S(2)}, u32[]{:S(2)}) collective-permute-start(f32[5,4,6,128]{3,2,1,0:T(8,128)S(1)} %get-tuple-element.15), channel_id=1, source_target_pairs={{0,16},{16,32},{32,48},{48,64},{64,80},{80,96},{96,112},{112,128},... | collective-permute-start | bytes 184328 | tf_op jit(solution)/shard_map/ppermute | solution.py:311
  57.1 4.5 %copy-start.2 = (f32[1024]{0:T(1024)S(1)}, f32[1024]{0:T(1024)}, u32[]{:S(2)}) copy-start(f32[1024]{0:T(1024)} %param.8) | copy-start | bytes 12292
  57.1 4.5 %copy-start.3 = (f32[1024]{0:T(1024)S(1)}, f32[1024]{0:T(1024)}, u32[]{:S(2)}) copy-start(f32[1024]{0:T(1024)} %param.7) | copy-start | bytes 12292
  57.1 4.5 %copy-start.1 = (f32[4,1024]{1,0:T(4,128)S(1)}, f32[4,1024]{1,0:T(4,128)}, u32[]{:S(2)}) copy-start(f32[4,1024]{1,0:T(4,128)} %param.9) | copy-start | bytes 49156
  57.1 4.8 %copy-start.4 = (s32[1024]{0:T(1024)S(1)}, s32[1024]{0:T(1024)}, u32[]{:S(2)}) copy-start(s32[1024]{0:T(1024)} %param.6) | copy-start | bytes 12292
  57.1 18.4 %all-to-all-start.1 = ((f32[4,592,128]{2,1,0:T(8,128)}), f32[4,592,128]{2,1,0:T(8,128)S(1)}, u32[]{:S(2)}, u32[]{:S(2)}) async-start(f32[4,592,128]{2,1,0:T(8,128)} %spread.1), calls=%async_computation.1 | async-start | bytes 2424832 | tf_op jit(solution)/shard_map/all_to_all | solution.py:352

commit v7 on v6

--- a/solution.py
+++ b/solution.py
@@ -69,7 +69,12 @@
     return start * (1.0 / 3.0) + (2.0 / 3.0) * (now + change)
 
 
-def row_values(rows_ref, coef_ref):
+def own_place():
+    ring = lax.axis_index("azi")
+    return 4 * (ring % 4) + ring // 4
+
+
+def row_values(rows_ref, coef_ref, around_ref):
     wide = 2 * LANES
     total = rows_ref.shape[1]
     row_start = lax.axis_index("rad") * ROWS
@@ -96,6 +101,9 @@
     local = row_start + jnp.where(local < ROWS + HALO, local, local - TALL)
     inside = (local >= 0) & (local < total)
     coef_ref[4 + LEVELS] = jnp.where(inside, 1.0, 0.0)
+    turn = lax.rem(TALL + REACH - own_place(), TALL)
+    for i in range(5 + LEVELS):
+        around_ref[i] = pltpu.roll(coef_ref[i], turn, 0)[0:8]
 
 
 def first_step(
@@ -197,14 +205,16 @@
     return jnp.where(lane >= offset, near, far)
 
 
-def second_step(amount_ref, coef_ref, got_ref, send_ref, begin, one, two):
+def second_step(shift_ref, coef_ref, got_ref, send_ref, begin, one, two):
     lane = lax.broadcasted_iota(jnp.int32, (16, LANES), 1)
     edge = (lane < REACH) | (lane >= LANES - REACH)
     leftward = lax.rem(lane, HALO) < REACH
     span = 1 + HALO
+    own_row = lax.axis_index("rad") * ROWS + own_place()
+    last = shift_ref.shape[0] - 1
 
     def take(row, carry):
-        amount = amount_ref[row]
+        amount = shift_ref[jnp.clip(own_row - REACH + row, 0, last)]
         first = row * HELD
         spill = got_ref[pl.ds(first + PLANES, 16, BAND), :]
         spill = jnp.where(
@@ -221,12 +231,15 @@
 
     sources = (begin, one, two)
     targets = (one, two, None)
-    last_amount = amount_ref[REACH]
+    last_amount = shift_ref[own_row]
     for stage in range(3):
         src, dst = sources[stage], targets[stage]
 
         def section(row):
-            scalars = [coef_ref[row, i] for i in range(5 + LEVELS)]
+            scalars = [
+                jnp.broadcast_to(coef_ref[i, row : row + 1, :], (16, LANES))
+                for i in range(5 + LEVELS)
+            ]
             inside = scalars[4 + LEVELS] > 0.5
             for k in range(LEVELS):
 
@@ -297,14 +310,14 @@
 
 def on_device(state, shifts, spin, drift, stiffness):
     rad = lax.axis_size("rad")
-    ring = lax.axis_index("azi")
-    total = spin.shape[0]
-    row_start = lax.axis_index("rad") * ROWS
-
     few = f32(FIELDS, LEVELS, HALO, LANES)
     low, high, state = call(cut, (few, few, f32(*state.shape)), [VMEM])(state)
     named = [spin[None], drift[None], stiffness]
-    coefs = call(row_values, f32(5 + LEVELS, TALL, LANES), [VMEM])(
+    coefs, around = call(
+        row_values,
+        (f32(5 + LEVELS, TALL, LANES), f32(5 + LEVELS, 8, LANES)),
+        [VMEM],
+    )(
         jnp.concatenate(named + named[0:2], axis=0)
     )
     below = lax.ppermute(low, "rad", [(i + 1, i) for i in range(rad - 1)])
@@ -324,36 +337,11 @@
     got = lax.all_to_all(sent, "azi", 0, 0, axis_index_groups=along_z)
     sent = call(spread, f32(4, 4 * BAND, LANES), [VMEM])(got)
 
-    spin, drift, stiffness, shifts, sent = lax.optimization_barrier(
-        (spin, drift, stiffness, shifts, sent)
-    )
-    own_row = row_start + 4 * (ring % 4) + ring // 4
-    rows = jnp.concatenate(
-        [
-            jnp.stack(
-                [
-                    NEAR - HD * drift,
-                    NEAR + HD * drift,
-                    (2.0 * DT) * spin,
-                    (0.5 * DT) * spin,
-                ]
-            ),
-            stiffness,
-            jnp.ones((1, total), jnp.float32),
-        ],
-        axis=0,
-    )
-    rows = jnp.pad(rows, ((0, 0), (REACH, REACH)))
-    around = lax.dynamic_slice_in_dim(rows, own_row, 1 + HALO, axis=1).T
-    turn = lax.dynamic_slice_in_dim(
-        jnp.pad(shifts, (REACH, REACH)), own_row, 1 + HALO, axis=0
-    )
-
     got = lax.all_to_all(sent, "azi", 0, 0, axis_index_groups=along_x)
     band = pltpu.VMEM((1 + HALO, PLANES, 16, LANES), jnp.float32)
     sent = call(
-        second_step, f32(16 * PLANES, LANES), [SMEM, SMEM, VMEM], (band, band, band)
-    )(turn, around, got.reshape(16 * BAND, LANES))
+        second_step, f32(16 * PLANES, LANES), [SMEM, VMEM, VMEM], (band, band, band)
+    )(shifts, around, got.reshape(16 * BAND, LANES))
     got = lax.all_to_all(sent.reshape(16, FIELDS, LEVELS, LANES), "azi", 0, 0)
     return call(set_down, f32(FIELDS, LEVELS, ROWS, LANES), [VMEM])(
         got.reshape(16 * PLANES, LANES)

time: 104 us -> 103 us (level)
  blocking collectives: 61 us -> 78.6 us
  waiting for transfers between devices: 19 us -> 5.44 us
  starting transfers between devices: 14.5 us -> 10 us
    all_to_all x0 -> x1, blocking collectives: none -> 18.1 us  [on_device(): got = lax.all_to_all(sent, 'azi', 0, 0, axis_index_groups=along_x)]
    all_to_all x1 -> x0, waiting for transfers between devices: 13.5 us -> none  [on_device(): got = lax.all_to_all(sent, 'azi', 0, 0, axis_index_groups=along_x)]
    all_to_all x1 -> x0, starting transfers between devices: 4.44 us -> none  [on_device(): got = lax.all_to_all(sent, 'azi', 0, 0, axis_index_groups=along_x)]
  transfers between devices with their start and end apart: 3 -> 2, of which waited for: 2 -> 1; matrix products, arithmetic and copies ran while one was open for 1% -> 1% of each run, Pallas kernels for 0% -> 0%
where the time goes in v7:
time: 103 us; the launch traced here: 102 us
  blocking collectives  78.6 us (76%)
  starting transfers between devices  10 us (10%)
  Pallas kernels  6.02 us (6%)
  waiting for transfers between devices  5.44 us (5%)
  local copies, waits for them, and re-layouts  1.73 us (2%)
    all_to_all x1, blocking collectives, on_device(): got = lax.all_to_all(sent, 'azi', 0, 0, axis_index_groups=along_z)  36.7 us
    all_to_all x1, blocking collectives, on_device(): got = lax.all_to_all(sent.reshape(16, FIELDS, LEVELS, LANES), 'azi', 0, 0)  23.9 us
    all_to_all x1, blocking collectives, on_device(): got = lax.all_to_all(sent, 'azi', 0, 0, axis_index_groups=along_x)  18.1 us
    ppermute x1, starting transfers between devices, on_device(): below = lax.ppermute(low, 'rad', [(i + 1, i) for i in range(rad - 1)])  8.12 us
    ppermute x1, waiting for transfers between devices, on_device(): above = lax.ppermute(high, 'rad', [(i, i + 1) for i in range(rad - 1)])  5.44 us
    pallas_call x1, Pallas kernels, on_device(): call(second_step, f32(16 * PLANES, LANES), [SMEM, VMEM, VMEM], (band, ban...  3.14 us
  transfers between devices with their start and end apart: 2, of which 1 were waited for; matrix products, arithmetic and copies ran while one was open for 1% of the time, Pallas kernels for 0%

profile of v7, /device:TPU:56, one launch (start us, length us, event | category | flops | bytes accessed | tf_op | source)
XLA Modules:
  0.0 101.9 jit_solution(1390523801304227167)
XLA Ops:
  0.0 0.0 copy-start
  0.0 0.9 copy-done
  0.9 8.1 %collective-permute-start = (f32[5,4,6,128]{3,2,1,0:T(8,128)S(1)}, f32[5,4,6,128]{3,2,1,0:T(8,128)S(1)}, u32[]{:S(2)}, u32[]{:S(2)}) collective-permute-start(f32[5,4,6,128]{3,2,1,0:T(8,128)S(1)} %get-tuple-element.12), channel_id=1, source_target_pairs={{16,0},{32,16},{48,32},{64,48},{80,64},{96,80},{112,96},{128,112},... | collective-permute-start | bytes 184328 | tf_op jit(solution)/shard_map/ppermute | solution.py:323
  9.1 1.9 %collective-permute-start.1 = (f32[5,4,6,128]{3,2,1,0:T(8,128)S(1)}, f32[5,4,6,128]{3,2,1,0:T(8,128)S(1)}, u32[]{:S(2)}, u32[]{:S(2)}) collective-permute-start(f32[5,4,6,128]{3,2,1,0:T(8,128)S(1)} %get-tuple-element.13), channel_id=1, source_target_pairs={{0,16},{16,32},{32,48},{48,64},{64,80},{80,96},{96,112},{112,128},... | collective-permute-start | bytes 184328 | tf_op jit(solution)/shard_map/ppermute | solution.py:324
  11.0 0.8 concatenate.3.rows_ref
  11.8 0.3 row_values.1
  12.1 0.0 collective-permute-done.below_ref
  12.1 5.4 %collective-permute-done.1.above_ref = f32[5,4,6,128]{3,2,1,0:T(8,128)S(1)} collective-permute-done((f32[5,4,6,128]{3,2,1,0:T(8,128)S(1)}, f32[5,4,6,128]{3,2,1,0:T(8,128)S(1)}, u32[]{:S(2)}, u32[]{:S(2)}) %collective-permute-start.1) | collective-permute-done | bytes 61472 | tf_op jit(solution)/shard_map/ppermute | solution.py:324
  17.5 1.8 %first_step.1 = f32[4,216,128]{2,1,0:T(8,128)S(1)} custom-call(f32[5,4,16,128]{3,2,1,0:T(8,128)S(1)} %get-tuple-element.11.main_ref, f32[5,4,6,128]{3,2,1,0:T(8,128)S(1)} %collective-permute-done.below_ref, f32[5,4,6,128]{3,2,1,0:T(8,128)S(1)} %collective-permute-done.1.above_ref, f32[9,32,128]{2,1,0:T(8,128)S(1)} %get-tuple-element.14.coef_ref), custom_call_target="tpu_custom_call" | custom-call | tf_op jit(solution)/shard_map/first_step/pallas_call | solution.py:329
  19.3 36.7 %all_to_all.15.got_ref = f32[4,216,128]{2,1,0:T(8,128)S(1)} all-to-all(f32[4,216,128]{2,1,0:T(8,128)S(1)} %first_step.1), channel_id=1, replica_groups={{0,1,2,3},{4,5,6,7},{8,9,10,11},{12,13,14,15},{16,17,18,19},{20,21,22,2..., dimensions={0} | all-to-all | bytes 884736 | tf_op jit(solution)/shard_map/all_to_all | solution.py:337
  56.0 0.1 spread.1
  56.1 0.0 copy-start.1
  56.1 18.1 %all_to_all.16 = f32[4,592,128]{2,1,0:T(8,128)S(1)} all-to-all(f32[4,592,128]{2,1,0:T(8,128)S(1)} %spread.1), channel_id=1, replica_groups={{0,4,8,12},{1,5,9,13},{2,6,10,14},{3,7,11,15},{16,20,24,28},{17,21,25,2..., dimensions={0} | all-to-all | bytes 2424832 | tf_op jit(solution)/shard_map/all_to_all | solution.py:340
  74.2 0.0 copy-done.1
  74.2 3.1 %second_step.1 = f32[320,128]{1,0:T(8,128)S(1)} custom-call(s32[1024]{0:T(1024)S(1)} %copy-done.1, f32[9,8,128]{2,1,0:T(8,128)S(1)} %get-tuple-element.10.coef_ref, f32[2368,128]{1,0:T(8,128)S(1)} %bitcast.5), custom_call_target="tpu_custom_call" | custom-call | tf_op jit(solution)/shard_map/second_step/pallas_call | solution.py:342
  77.3 23.9 %all_to_all.17 = f32[16,5,4,128]{3,2,1,0:T(4,128)S(1)} all-to-all(f32[16,5,4,128]{3,2,1,0:T(4,128)S(1)} %bitcast.7), channel_id=1, replica_groups=mesh['rad'=64,'azi'=16] {'azi'}, dimensions={0} | all-to-all | bytes 327680 | tf_op jit(solution)/shard_map/all_to_all | solution.py:345
  101.2 0.7 set_down.1
  (1 shorter events, 0.0 us)
Async XLA Ops:
  0.0 0.9 copy-start
  0.9 11.1 %collective-permute-start = (f32[5,4,6,128]{3,2,1,0:T(8,128)S(1)}, f32[5,4,6,128]{3,2,1,0:T(8,128)S(1)}, u32[]{:S(2)}, u32[]{:S(2)}) collective-permute-start(f32[5,4,6,128]{3,2,1,0:T(8,128)S(1)} %get-tuple-element.12), channel_id=1, source_target_pairs={{16,0},{32,16},{48,32},{64,48},{80,64},{96,80},{112,96},{128,112},... | collective-permute-start | bytes 184328 | tf_op jit(solution)/shard_map/ppermute | solution.py:323
  9.1 8.5 %collective-permute-start.1 = (f32[5,4,6,128]{3,2,1,0:T(8,128)S(1)}, f32[5,4,6,128]{3,2,1,0:T(8,128)S(1)}, u32[]{:S(2)}, u32[]{:S(2)}) collective-permute-start(f32[5,4,6,128]{3,2,1,0:T(8,128)S(1)} %get-tuple-element.13), channel_id=1, source_target_pairs={{0,16},{16,32},{32,48},{48,64},{64,80},{80,96},{96,112},{112,128},... | collective-permute-start | bytes 184328 | tf_op jit(solution)/shard_map/ppermute | solution.py:324
  56.1 18.1 %copy-start.1 = (s32[1024]{0:T(1024)S(1)}, s32[1024]{0:T(1024)}, u32[]{:S(2)}) copy-start(s32[1024]{0:T(1024)} %shift_ref.1) | copy-start | bytes 12292

commit v8 on v7

--- a/solution.py
+++ b/solution.py
@@ -25,7 +25,7 @@
 ROOM = 16 * 1024 * 1024
 
 
-def cut(main_ref, low_ref, high_ref, kept_ref):
+def cut(main_ref, high_ref, low_ref, kept_ref):
     for plane in range(PLANES):
         f, k = divmod(plane, LEVELS)
         low_ref[f, k] = main_ref[f, k, 0:HALO]
@@ -108,8 +108,8 @@
 
 def first_step(
     main_ref,
+    above_ref,
     below_ref,
-    above_ref,
     coef_ref,
     send_ref,
     begin,
@@ -311,7 +311,7 @@
 def on_device(state, shifts, spin, drift, stiffness):
     rad = lax.axis_size("rad")
     few = f32(FIELDS, LEVELS, HALO, LANES)
-    low, high, state = call(cut, (few, few, f32(*state.shape)), [VMEM])(state)
+    high, low, state = call(cut, (few, few, f32(*state.shape)), [VMEM])(state)
     named = [spin[None], drift[None], stiffness]
     coefs, around = call(
         row_values,
@@ -320,8 +320,8 @@
     )(
         jnp.concatenate(named + named[0:2], axis=0)
     )
+    above = lax.ppermute(high, "rad", [(i, i + 1) for i in range(rad - 1)])
     below = lax.ppermute(low, "rad", [(i + 1, i) for i in range(rad - 1)])
-    above = lax.ppermute(high, "rad", [(i, i + 1) for i in range(rad - 1)])
 
     count = (4 + HALO) * HELD
     count += -count % 8
@@ -331,7 +331,7 @@
         f32(4, count, LANES),
         [VMEM] * 4,
         (tile, tile, tile, pltpu.VMEM((PACK * HELD, LANES), jnp.float32)),
-    )(state, below, above, coefs)
+    )(state, above, below, coefs)
     along_z = [[4 * x + z for z in range(4)] for x in range(4)]
     along_x = [[4 * x + z for x in range(4)] for z in range(4)]
     got = lax.all_to_all(sent, "azi", 0, 0, axis_index_groups=along_z)

time: 103 us -> 106 us (1.029)
  the two profiles are of different devices: /device:TPU:56 before, /device:TPU:96 now
where the time goes in v8:
time: 106 us
  blocking collectives  91.5 us (86%)
  Pallas kernels  6.02 us (6%)
  starting transfers between devices  5.56 us (5%)
  local copies, waits for them, and re-layouts  1.73 us (2%)
    all_to_all x1, blocking collectives, on_device(): got = lax.all_to_all(sent, 'azi', 0, 0, axis_index_groups=along_z)  45.4 us
    all_to_all x1, blocking collectives, on_device(): got = lax.all_to_all(sent.reshape(16, FIELDS, LEVELS, LANES), 'azi', 0, 0)  25.4 us
    all_to_all x1, blocking collectives, on_device(): got = lax.all_to_all(sent, 'azi', 0, 0, axis_index_groups=along_x)  20.7 us
    ppermute x1, starting transfers between devices, on_device(): below = lax.ppermute(low, 'rad', [(i + 1, i) for i in range(rad - 1)])  3.64 us
    pallas_call x1, Pallas kernels, on_device(): call(second_step, f32(16 * PLANES, LANES), [SMEM, VMEM, VMEM], (band, ban...  3.14 us
  transfers between devices with their start and end apart: 2, of which 1 were waited for; matrix products, arithmetic and copies ran while one was open for 1% of the time, Pallas kernels for 0%

profile of v8, /device:TPU:96, one launch (start us, length us, event | category | flops | bytes accessed | tf_op | source)
XLA Modules:
  0.0 105.8 jit_solution(9090159717430506574)
XLA Ops:
  0.0 0.0 copy-start
  0.0 0.9 copy-done
  0.9 1.9 %collective-permute-start = (f32[5,4,6,128]{3,2,1,0:T(8,128)S(1)}, f32[5,4,6,128]{3,2,1,0:T(8,128)S(1)}, u32[]{:S(2)}, u32[]{:S(2)}) collective-permute-start(f32[5,4,6,128]{3,2,1,0:T(8,128)S(1)} %get-tuple-element.12), channel_id=1, source_target_pairs={{0,16},{16,32},{32,48},{48,64},{64,80},{80,96},{96,112},{112,128},... | collective-permute-start | bytes 184328 | tf_op jit(solution)/shard_map/ppermute | solution.py:323
  2.9 3.6 %collective-permute-start.1 = (f32[5,4,6,128]{3,2,1,0:T(8,128)S(1)}, f32[5,4,6,128]{3,2,1,0:T(8,128)S(1)}, u32[]{:S(2)}, u32[]{:S(2)}) collective-permute-start(f32[5,4,6,128]{3,2,1,0:T(8,128)S(1)} %get-tuple-element.13), channel_id=1, source_target_pairs={{16,0},{32,16},{48,32},{64,48},{80,64},{96,80},{112,96},{128,112},... | collective-permute-start | bytes 184328 | tf_op jit(solution)/shard_map/ppermute | solution.py:324
  6.5 0.8 concatenate.3.rows_ref
  7.3 0.3 row_values.1
  7.6 0.0 collective-permute-done.above_ref
  7.6 0.9 collective-permute-done.1.below_ref
  8.6 1.8 %first_step.1 = f32[4,216,128]{2,1,0:T(8,128)S(1)} custom-call(f32[5,4,16,128]{3,2,1,0:T(8,128)S(1)} %get-tuple-element.11.main_ref, f32[5,4,6,128]{3,2,1,0:T(8,128)S(1)} %collective-permute-done.above_ref, f32[5,4,6,128]{3,2,1,0:T(8,128)S(1)} %collective-permute-done.1.below_ref, f32[9,32,128]{2,1,0:T(8,128)S(1)} %get-tuple-element.14.coef_ref), custom_call_target="tpu_custom_call" | custom-call | tf_op jit(solution)/shard_map/first_step/pallas_call | solution.py:329
  10.3 45.4 %all_to_all.15.got_ref = f32[4,216,128]{2,1,0:T(8,128)S(1)} all-to-all(f32[4,216,128]{2,1,0:T(8,128)S(1)} %first_step.1), channel_id=1, replica_groups={{0,1,2,3},{4,5,6,7},{8,9,10,11},{12,13,14,15},{16,17,18,19},{20,21,22,2..., dimensions={0} | all-to-all | bytes 884736 | tf_op jit(solution)/shard_map/all_to_all | solution.py:337
  55.8 0.1 spread.1
  55.9 0.0 copy-start.1
  55.9 20.7 %all_to_all.16 = f32[4,592,128]{2,1,0:T(8,128)S(1)} all-to-all(f32[4,592,128]{2,1,0:T(8,128)S(1)} %spread.1), channel_id=1, replica_groups={{0,4,8,12},{1,5,9,13},{2,6,10,14},{3,7,11,15},{16,20,24,28},{17,21,25,2..., dimensions={0} | all-to-all | bytes 2424832 | tf_op jit(solution)/shard_map/all_to_all | solution.py:340
  76.5 0.0 copy-done.1
  76.5 3.1 %second_step.1 = f32[320,128]{1,0:T(8,128)S(1)} custom-call(s32[1024]{0:T(1024)S(1)} %copy-done.1, f32[9,8,128]{2,1,0:T(8,128)S(1)} %get-tuple-element.10.coef_ref, f32[2368,128]{1,0:T(8,128)S(1)} %bitcast.5), custom_call_target="tpu_custom_call" | custom-call | tf_op jit(solution)/shard_map/second_step/pallas_call | solution.py:342
  79.7 25.4 %all_to_all.17 = f32[16,5,4,128]{3,2,1,0:T(4,128)S(1)} all-to-all(f32[16,5,4,128]{3,2,1,0:T(4,128)S(1)} %bitcast.7), channel_id=1, replica_groups=mesh['rad'=64,'azi'=16] {'azi'}, dimensions={0} | all-to-all | bytes 327680 | tf_op jit(solution)/shard_map/all_to_all | solution.py:345
  105.1 0.7 set_down.1
  (1 shorter events, 0.0 us)
Async XLA Ops:
  0.0 0.9 copy-start
  0.9 6.7 %collective-permute-start = (f32[5,4,6,128]{3,2,1,0:T(8,128)S(1)}, f32[5,4,6,128]{3,2,1,0:T(8,128)S(1)}, u32[]{:S(2)}, u32[]{:S(2)}) collective-permute-start(f32[5,4,6,128]{3,2,1,0:T(8,128)S(1)} %get-tuple-element.12), channel_id=1, source_target_pairs={{0,16},{16,32},{32,48},{48,64},{64,80},{80,96},{96,112},{112,128},... | collective-permute-start | bytes 184328 | tf_op jit(solution)/shard_map/ppermute | solution.py:323
  2.9 5.7 %collective-permute-start.1 = (f32[5,4,6,128]{3,2,1,0:T(8,128)S(1)}, f32[5,4,6,128]{3,2,1,0:T(8,128)S(1)}, u32[]{:S(2)}, u32[]{:S(2)}) collective-permute-start(f32[5,4,6,128]{3,2,1,0:T(8,128)S(1)} %get-tuple-element.13), channel_id=1, source_target_pairs={{16,0},{32,16},{48,32},{64,48},{80,64},{96,80},{112,96},{128,112},... | collective-permute-start | bytes 184328 | tf_op jit(solution)/shard_map/ppermute | solution.py:324
  55.9 20.7 %copy-start.1 = (s32[1024]{0:T(1024)S(1)}, s32[1024]{0:T(1024)}, u32[]{:S(2)}) copy-start(s32[1024]{0:T(1024)} %shift_ref.1) | copy-start | bytes 12292
